TPU v7x, 512 devices: a whole 4x4x16 slice. The times are simulated.
512 devices in a mesh: table: 64 (over y, z), dp: 8 (over x, core).
Axes of the slice: x: 4, y: 4, z: 16, core: 2. Of those that a mesh axis runs over, the one named last changes fastest.
Arguments:
- emb_table: float32 [131072, 128], P('table'), may hold values from -4 to 4
- versions: int32 [131072], P('table'), may hold values from 0 to 999
- conf_local: int32 [16384], P('table'), may hold values from 0 to 2047, as said below
- conf_version: int32 [16384], P('table'), may hold values from 0 to 999
- conf_values: float32 [16384, 128], P('table'), may hold values from -4 to 4
- owners: int32 [65536, 26, 1], P(('table', 'dp')), may hold values from 0 to 63; in each aligned block of 3328 rows (0 to 3327, 3328 to 6655, ..., all dimensions but the last counted through in order) at most 78 rows name the same one
- row_local: int32 [65536, 26, 2], P(('table', 'dp')), may hold values from 0 to 2047
- lengths: int32 [65536, 26], P(('table', 'dp')), may hold values from 1 to 2
- dense_out: bfloat16 [65536, 128], P(('table', 'dp')), may hold values from -6 to 6
- labels: int32 [65536], P(('table', 'dp')), may hold values 0 or 1
- cross_down: bfloat16 [1, 3456, 512], P(None, None, 'dp'), may hold values from -0.109375 to 0.109375
- cross_up: bfloat16 [1, 512, 3456], P(None, 'dp'), may hold values from -0.25 to 0.25
- cross_bias: float32 [1, 3456], replicated, may hold values from -3 to 3
- head_weight: float32 [3456], replicated, may hold values from -0.109375 to 0.109375
Outputs:
- logits: float32 [65536], P(('table', 'dp'))
- emb_grad: float32 [131072, 128], P(('table', 'dp'))
Inputs may be any that keep to these rules, and one draw needn't show every extreme that they name: `owners`: in each aligned block of the 3328 bags of one device (samples in order, bags within a sample in order), at most 78 bags name one holder; in some block one holder is named by exactly 78 bags. `conf_local`: within each holder's 256 entries the local row numbers are distinct.
All inputs are finite; a program needn't handle non-finite values. No bound on the sum of `labels` on one device may be relied on, other than what follows from the above.
Results may differ from a plain program's by a relative error of at most 0.0035.
Values may be sent and summed in bfloat16 or wider, within the bound.
A program may use at most 64 MiB of HBM per device.

v0:
```python
import jax
import jax.numpy as jnp
from jax import lax
from jax.sharding import PartitionSpec as P

loss_scale = 64.0


def dense_step(inputs, labels, cross_down, cross_up, cross_bias, head_weight):
    base_float = inputs.astype(jnp.float32)
    state = base_float
    cross_index = 0
    crossed = jnp.dot(inputs, cross_down[cross_index], preferred_element_type=jnp.float32).astype(
        jnp.bfloat16
    )
    factor = (
        jnp.dot(crossed, cross_up[cross_index], preferred_element_type=jnp.float32)
        + cross_bias[cross_index]
    )
    factors = [factor]
    state = base_float * factor + state
    logits = jnp.sum(state * head_weight, axis=1)
    signal = loss_scale * (jax.nn.sigmoid(logits) - labels.astype(jnp.float32))
    grad_state = signal[:, None] * head_weight[None, :]
    cross_index = 0
    grad_base = grad_state * factors[cross_index]
    grad_lift = (grad_state * base_float).astype(jnp.bfloat16)
    grad_cross = lax.dot_general(
        grad_lift,
        cross_up[cross_index],
        (((1,), (1,)), ((), ())),
        preferred_element_type=jnp.float32,
    ).astype(jnp.bfloat16)
    grad_state = grad_state + lax.dot_general(
        grad_cross,
        cross_down[cross_index],
        (((1,), (1,)), ((), ())),
        preferred_element_type=jnp.float32,
    )
    return (logits, grad_state + grad_base)


def body(
    emb_table,
    versions,
    conf_local,
    conf_version,
    conf_values,
    owners,
    row_local,
    lengths,
    dense_out,
    labels,
    cross_down,
    cross_up,
    cross_bias,
    head_weight,
):
    peers = lax.axis_size("table")
    rows_dev, emb_width = emb_table.shape
    is_newer = conf_version > versions[conf_local]
    current = emb_table[conf_local]
    updated = emb_table.at[conf_local].set(jnp.where(is_newer[:, None], conf_values, current))
    samples, features, slot_count = row_local.shape
    bag_count = samples * features
    capacity = 3 * bag_count // (2 * peers)
    owner_flat = owners.reshape(bag_count)
    onehot_owner = (owner_flat[:, None] == jnp.arange(peers, dtype=jnp.int32)[None, :]).astype(
        jnp.int32
    )
    earlier = jnp.cumsum(onehot_owner, axis=0) - onehot_owner
    rank_in_owner = jnp.sum(earlier * onehot_owner, axis=1)
    position = owner_flat * capacity + rank_in_owner
    request_rows = (
        jnp.zeros((peers * capacity, slot_count), jnp.int32)
        .at[position]
        .set(row_local.reshape(bag_count, slot_count))
    )
    request_rows = request_rows.reshape(peers, capacity, slot_count)
    request_len = (
        jnp.zeros((peers * capacity,), jnp.int32).at[position].set(lengths.reshape(bag_count))
    )
    request_len = request_len.reshape(peers, capacity)
    slot_index = jnp.arange(slot_count, dtype=jnp.int32)
    asked_rows = lax.all_to_all(request_rows, "table", split_axis=0, concat_axis=0, tiled=True)
    asked_len = lax.all_to_all(request_len, "table", split_axis=0, concat_axis=0, tiled=True)
    live_mask = slot_index[None, None, :] < asked_len[:, :, None]
    looked_up = jnp.where(live_mask[..., None], updated[asked_rows], 0.0)
    answer = lax.all_to_all(looked_up, "table", split_axis=0, concat_axis=0, tiled=True)
    answer, got_rows, got_len = (answer, asked_rows, asked_len)
    slot_pooled = jnp.sum(answer, axis=2)
    pooled = slot_pooled.reshape(peers * capacity, emb_width)[position].reshape(
        samples, features * emb_width
    )
    inputs = jnp.concatenate([dense_out.astype(jnp.float32), pooled], axis=1).astype(jnp.bfloat16)
    full_down, full_up = (
        lax.all_gather(cross_down, "dp", axis=2, tiled=True),
        lax.all_gather(cross_up, "dp", axis=1, tiled=True),
    )
    logits, grad_input = dense_step(inputs, labels, full_down, full_up, cross_bias, head_weight)
    bag_grad = grad_input[:, emb_width:].reshape(bag_count, emb_width)
    send_grad = jnp.zeros((peers * capacity, emb_width), jnp.float32).at[position].set(bag_grad)
    send_grad = send_grad.reshape(peers, capacity, emb_width)
    got_grad = lax.all_to_all(send_grad, "table", split_axis=0, concat_axis=0, tiled=True)
    live_held = slot_index[None, None, :] < got_len[:, :, None]
    updates = jnp.where(live_held[..., None], got_grad[:, :, None, :], 0.0)
    local_grad = (
        jnp.zeros((rows_dev, emb_width), jnp.float32)
        .at[got_rows.reshape(-1)]
        .add(updates.reshape(-1, emb_width))
    )
    emb_grad = lax.psum_scatter(local_grad, "dp", scatter_dimension=0, tiled=True)
    return (logits, emb_grad)


def solution(mesh):
    in_specs = (
        P("table", None),
        P("table"),
        P("table"),
        P("table"),
        P("table", None),
        P(("table", "dp"), None, None),
        P(("table", "dp"), None, None),
        P(("table", "dp"), None),
        P(("table", "dp"), None),
        P(("table", "dp")),
        P(None, None, "dp"),
        P(None, "dp", None),
        P(),
        P(),
    )
    out_specs = (P(("table", "dp")), P(("table", "dp"), None))
    return jax.shard_map(body, mesh=mesh, in_specs=in_specs, out_specs=out_specs, check_vma=False)
```

profile of v0, /device:TPU:1, one launch (start us, length us, event | category | flops | bytes accessed | tf_op | source)
XLA Modules:
  0.0 677.2 jit_solution(11305970535627712777)
XLA Ops:
  7.2 0.8 copy.37
  8.3 0.7 broadcast_multiply_fusion.3
  9.1 18.4 %reduce-window.6 = s32[64,26,128]{2,1,0:T(8,128)S(1)} reduce-window(s32[64,26,128]{2,1,0:T(8,128)S(1)} %fusion.27, s32[]{:T(128)} %constant.7.clone.1), window={size=1x1x128 pad=0_0x0_0x127_0}, to_apply=%region_0.1 | reduce-window | flops 27049984 | bytes 1703940 | tf_op jit(solution)/shard_map/reduce-window
  27.9 0.5 copy.48
  29.5 0.7 fusion.34
  30.2 12.7 %scatter_custom_fusion = s32[4992]{0:T(1024)S(1)} fusion(s32[3328]{0:T(1024)S(1)} %fusion.40, s32[3328]{0:T(1024)S(1)} %reshape.168, s32[]{:T(128)} %constant.7.clone.1), kind=kCustom, calls=%fused_computation.57 | custom fusion | bytes 19972 | tf_op jit(solution)/shard_map/scatter | solution.py:81
  43.0 0.8 all_to_all.15
  43.7 19.3 %all-to-all-start = ((s32[64,1,78]{2,1,0:T(1,128)}), s32[64,1,78]{2,1,0:T(1,128)S(1)}, u32[]{:S(2)}, u32[]{:S(2)}) async-start(s32[64,1,78]{2,1,0:T(1,128)} %all_to_all.15), calls=%async_computation | async-start | bytes 65536 | tf_op jit(solution)/shard_map/all_to_all | solution.py:86
  63.3 0.5 copy.43
  63.9 14.9 %scatter_custom_fusion.2 = s32[4992,2]{1,0:T(8,128)} fusion(s32[3328]{0:T(1024)S(1)} %fusion.40, s32[3328,2]{1,0:T(8,128)S(1)} %copy.43, s32[]{:T(128)} %constant.7.clone.1), kind=kCustom, calls=%fused_computation.33 | custom fusion | bytes 39940 | tf_op jit(solution)/shard_map/scatter | solution.py:77
  78.8 2.6 copy.44
  81.6 0.7 copy.45
  82.3 1.7 gather_fusion
  84.0 2.1 scatter_custom_fusion.1
  86.2 14.8 %all-to-all-start.1 = ((s32[64,78,2]{1,2,0:T(2,128)}), s32[64,78,2]{1,2,0:T(2,128)S(1)}, u32[]{:S(2)}, u32[]{:S(2)}) async-start(s32[64,78,2]{1,2,0:T(2,128)} %copy.45), calls=%async_computation.1 | async-start | bytes 131072 | tf_op jit(solution)/shard_map/all_to_all | solution.py:85
  100.9 1.0 iota_compare_fusion
  102.0 12.3 %all-to-all-done.1 = s32[64,78,2]{1,2,0:T(2,128)S(1)} async-done(((s32[64,78,2]{1,2,0:T(2,128)}), s32[64,78,2]{1,2,0:T(2,128)S(1)}, u32[]{:S(2)}, u32[]{:S(2)}) %all-to-all-start.1) | async-done | bytes 39968 | tf_op jit(solution)/shard_map/all_to_all | solution.py:85
  114.3 2.4 copy.46
  116.7 2.5 reshape.150
  119.2 19.1 %gather_fusion.1 = f32[9984,128]{1,0:T(8,128)} fusion(f32[2048,128]{1,0:T(8,128)S(1)} %scatter_custom_fusion.1, s32[10240]{0:T(1024)S(1)} %pad_clamp_fusion), kind=kCustom, calls=%fused_computation.2 | custom fusion | bytes 10263552 | tf_op jit(solution)/shard_map/gather | solution.py:88
  138.3 9.7 %broadcast_select_fusion = f32[64,78,2,128]{3,2,1,0:T(2,128)} fusion(f32[64,78,2,128]{3,2,1,0:T(2,128)} %bitcast.56, pred[64,78,2]{2,1,0:T(8,128)(4,1)S(1)} %iota_compare_fusion), kind=kLoop, calls=%fused_computation.11 | loop fusion | flops 1277952 | bytes 10233600 | tf_op jit(solution)/shard_map/jit(_where)/select_n | solution.py:88
  148.0 5.8 all-to-all-start.2
  153.9 0.7 all-gather.3.cloned.1.call-update
  154.7 0.7 all-gather.5.cloned.1.call-update
  155.4 0.6 reduce.1
  156.0 220.9 %all-to-all-done.2 = f32[64,78,2,128]{3,2,1,0:T(2,128)} async-done(((f32[64,78,2,128]{3,2,1,0:T(2,128)}), f32[64,78,2,128]{3,2,1,0:T(2,128)}, u32[]{:S(2)}, u32[]{:S(2)}) %all-to-all-start.2) | async-done | bytes 5111840 | tf_op jit(solution)/shard_map/all_to_all | solution.py:89
  376.9 8.7 %reduce_sum.31 = bf16[64,78,128]{2,1,0:T(8,128)(2,1)S(1)} reduce(f32[64,78,2,128]{3,2,1,0:T(2,128)} %all-to-all-done.2, f32[]{:T(128)} %constant.11.clone.1), dimensions={2}, to_apply=%region_6.7 | reduce | flops 638976 | bytes 6389764 | tf_op jit(solution)/shard_map/reduce_sum | solution.py:91
  385.6 0.6 reshape.127
  386.2 6.5 gather_fusion.2
  392.7 0.9 reshape.128
  393.8 0.9 copy-done.6
  394.7 7.4 %fusion.13 = (f32[128]{0:T(128)}, f32[128,3456]{1,0:T(8,128)}) fusion(bf16[128,3456]{1,0:T(8,128)(2,1)} %copy-done.6, f32[3456]{0:T(1024)S(1)} %copy-done.9, f32[3456]{0:T(1024)} %reduce.1, bf16[1,512,3456]{2,1,0:T(8,128)(2,1)} %all-gather.5.cloned.1.call-done, bf16[1,3456,512]{1,2,0:T(8,128)(2,1)} %all-gather.3.cloned.1.call-done), kind=kOutput, calls=%fused_computation.27 | convolution fusion | flops 908689280 | bytes 9760256 | tf_op jit(solution)/shard_map/dot_general | solution.py:17
  402.1 0.7 fusion.43
  402.8 0.5 copy-done.16
  403.3 1.4 broadcast_multiply_fusion
  404.7 5.4 fusion.5
  410.1 2.7 fusion.14
  412.8 1.3 reshape.192
  414.1 14.1 %scatter_custom_fusion.3 = f32[4992,128]{1,0:T(8,128)S(1)} fusion(s32[3328]{0:T(1024)} %copy-done.11, f32[3328,128]{1,0:T(8,128)} %reshape.192, f32[]{:T(128)} %constant.11.clone.1), kind=kCustom, calls=%fused_computation.31 | custom fusion | bytes 2556416 | tf_op jit(solution)/shard_map/scatter | solution.py:102
  428.2 1.6 reshape.131
  429.8 11.5 %all-to-all-start.3 = ((f32[64,78,128]{2,1,0:T(8,128)}), f32[64,78,128]{2,1,0:T(8,128)}, u32[]{:S(2)}, u32[]{:S(2)}) async-start(f32[64,78,128]{2,1,0:T(8,128)} %reshape.131), calls=%async_computation.3 | async-start | bytes 5242880 | tf_op jit(solution)/shard_map/all_to_all | solution.py:104
  441.6 0.8 lt.77
  442.4 1.0 copy.47
  443.5 0.9 reshape.129
  444.5 111.2 %all-to-all-done.3 = f32[64,78,128]{2,1,0:T(8,128)} async-done(((f32[64,78,128]{2,1,0:T(8,128)}), f32[64,78,128]{2,1,0:T(8,128)}, u32[]{:S(2)}, u32[]{:S(2)}) %all-to-all-start.3) | async-done | bytes 2555936 | tf_op jit(solution)/shard_map/all_to_all | solution.py:104
  555.7 5.7 broadcast_in_dim.89
  561.4 63.2 %scatter_custom_fusion.4 = f32[2048,128]{1,0:T(8,128)} fusion(s32[9984]{0:T(1024)S(1)} %fusion.39, f32[9984,128]{1,0:T(8,128)} %bitcast.57, f32[]{:T(128)} %constant.11.clone.1, pred[9984]{0:T(1024)(128)(4,1)S(1)} %lt.77), kind=kCustom, calls=%fused_computation.9 | custom fusion | flops 2555904 | bytes 6171648 | tf_op jit(solution)/shard_map/scatter-add | solution.py:110
  624.6 46.0 %reduce-scatter.2.cloned.1.call-done = f32[256,128]{1,0:T(8,128)} async-done(((f32[2048,128]{1,0:T(8,128)}), f32[256,128]{1,0:T(8,128)}) %reduce-scatter.2.cloned.1.call-update) | async-done | bytes 131088 | tf_op jit(solution)/shard_map/reduce_scatter | solution.py:112
  (66 shorter events, 3.0 us)
Async XLA Ops:
  7.2 75.1 %copy-start = (s32[2048]{0:T(1024)S(1)}, s32[2048]{0:T(1024)}, u32[]{:S(2)}) copy-start(s32[2048]{0:T(1024)} %param.15) | copy-start | bytes 24580
  27.6 1.6 copy-start.14
  27.9 35.1 %copy-start.13 = (s32[128,26,2]{0,2,1:T(2,128)S(1)}, s32[128,26,2]{0,2,1:T(2,128)}, u32[]{:S(2)}) copy-start(s32[128,26,2]{0,2,1:T(2,128)} %param.20) | copy-start | bytes 79876
  30.2 125.8 %copy-start.11 = (s32[3328]{0:T(1024)}, s32[3328]{0:T(1024)S(1)}, u32[]{:S(2)}) copy-start(s32[3328]{0:T(1024)S(1)} %fusion.40) | copy-start | bytes 39940
  43.7 42.4 %all-to-all-start = ((s32[64,1,78]{2,1,0:T(1,128)}), s32[64,1,78]{2,1,0:T(1,128)S(1)}, u32[]{:S(2)}, u32[]{:S(2)}) async-start(s32[64,1,78]{2,1,0:T(1,128)} %all_to_all.15), calls=%async_computation | async-start | bytes 65536 | tf_op jit(solution)/shard_map/all_to_all | solution.py:86
  63.9 18.4 %copy-start.17 = (s32[256]{0:T(256)S(1)}, s32[256]{0:T(256)}, u32[]{:S(2)}) copy-start(s32[256]{0:T(256)} %param.16) | copy-start | bytes 3076
  78.8 5.2 copy-start.18
  78.8 5.2 copy-start.2
  78.8 5.2 copy-start.10
  86.2 28.1 %all-to-all-start.1 = ((s32[64,78,2]{1,2,0:T(2,128)}), s32[64,78,2]{1,2,0:T(2,128)S(1)}, u32[]{:S(2)}, u32[]{:S(2)}) async-start(s32[64,78,2]{1,2,0:T(2,128)} %copy.45), calls=%async_computation.1 | async-start | bytes 131072 | tf_op jit(solution)/shard_map/all_to_all | solution.py:85
  102.0 36.4 %copy-start.4 = (pred[64,78,2]{2,1,0:T(8,128)(4,1)}, pred[64,78,2]{2,1,0:T(8,128)(4,1)S(1)}, u32[]{:S(2)}) copy-start(pred[64,78,2]{2,1,0:T(8,128)(4,1)S(1)} %iota_compare_fusion) | copy-start | bytes 29956
  114.3 4.9 copy-start.7
  148.0 7.3 %copy-start.15 = (f32[1,3456]{1,0:T(1,128)S(1)}, f32[1,3456]{1,0:T(1,128)}, u32[]{:S(2)}) copy-start(f32[1,3456]{1,0:T(1,128)} %param.26) | copy-start | bytes 41476
  148.0 8.0 %copy-start.12 = (bf16[128,128]{1,0:T(8,128)(2,1)S(1)}, bf16[128,128]{1,0:T(8,128)(2,1)}, u32[]{:S(2)}) copy-start(bf16[128,128]{1,0:T(8,128)(2,1)} %param.22) | copy-start | bytes 98308
  148.0 228.9 %all-to-all-start.2 = ((f32[64,78,2,128]{3,2,1,0:T(2,128)}), f32[64,78,2,128]{3,2,1,0:T(2,128)}, u32[]{:S(2)}, u32[]{:S(2)}) async-start(f32[64,78,2,128]{3,2,1,0:T(2,128)} %broadcast_select_fusion), calls=%async_computation.2 | async-start | bytes 10223616 | tf_op jit(solution)/shard_map/all_to_all | solution.py:89
  153.9 239.9 %all-gather.3.cloned.1.call-start = ((), (), s32[]{:S(2)}) async-start(), calls=%async_computation.5 | async-start | bytes 3981312 | tf_op jit(solution)/shard_map/all_gather | solution.py:97
  154.6 240.1 %all-gather.5.cloned.1.call-start = ((), (), s32[]{:S(2)}) async-start(), calls=%async_computation.6 | async-start | bytes 3981312 | tf_op jit(solution)/shard_map/all_gather | solution.py:98
  392.7 2.0 copy-start.9
  393.7 0.9 copy-start.6
  394.7 10.0 %copy-start.3 = (bf16[1,3456,512]{1,2,0:T(8,128)(2,1)S(1)}, bf16[1,3456,512]{1,2,0:T(8,128)(2,1)}, u32[]{:S(2)}) copy-start(bf16[1,3456,512]{1,2,0:T(8,128)(2,1)} %all-gather.3.cloned.1.call-done) | copy-start | bytes 10616836
  402.8 0.5 copy-start.16
  429.8 11.8 %copy-start.5 = (pred[64,78,2]{2,1,0:T(8,128)(4,1)S(1)}, pred[64,78,2]{2,1,0:T(8,128)(4,1)}, u32[]{:S(2)}) copy-start(pred[64,78,2]{2,1,0:T(8,128)(4,1)} %copy-done.4) | copy-start | bytes 29956
  429.8 12.6 %copy-start.8 = (s32[64,78,2]{1,2,0:T(2,128)S(1)}, s32[64,78,2]{1,2,0:T(2,128)}, u32[]{:S(2)}) copy-start(s32[64,78,2]{1,2,0:T(2,128)} %copy-done.7) | copy-start | bytes 119812
  429.8 125.8 %all-to-all-start.3 = ((f32[64,78,128]{2,1,0:T(8,128)}), f32[64,78,128]{2,1,0:T(8,128)}, u32[]{:S(2)}, u32[]{:S(2)}) async-start(f32[64,78,128]{2,1,0:T(8,128)} %reshape.131), calls=%async_computation.3 | async-start | bytes 5242880 | tf_op jit(solution)/shard_map/all_to_all | solution.py:104
  441.3 229.3 %reduce-scatter.2.cloned.1.call-start = ((), (), s32[]{:S(2)}) async-start(), calls=%async_computation.7 | async-start | bytes 1179648 | tf_op jit(solution)/shard_map/reduce_scatter | solution.py:112
  561.4 109.3 %copy-start.1 = (s32[2048]{0:T(1024)S(1)}, s32[2048]{0:T(1024)}, u32[]{:S(2)}) copy-start(s32[2048]{0:T(1024)} %param.15) | copy-start | bytes 24580
Sparse Core Ops, SparseCore 0:
  156.8 40.2 all-gather.2
  199.2 36.9 all-gather.4
  624.7 45.8 reduce-scatter.1
where the time goes:
time: 678 us; the launch traced here: 677 us
  waiting for transfers between devices  392 us (58%)
  other arithmetic  111 us (16%)
  local copies, waits for them, and re-layouts  95.8 us (14%)
  starting transfers between devices  51.7 us (8%)
  between operations  14.2 us (2%)
  matrix products  12.8 us (2%)
    all_to_all x1, waiting for transfers between devices, body(): lax.all_to_all(looked_up, 'table', split_axis=0, concat_axis=0, tiled=True)  221 us
    all_to_all x1, waiting for transfers between devices, body(): lax.all_to_all(send_grad, 'table', split_axis=0, concat_axis=0, tiled=True)  111 us
    scatter-add x1, other arithmetic, body(): local_grad = jnp.zeros((rows_dev, emb_width), jnp.float32).at[got_rows.re...  63.2 us
    reduce_scatter x1, waiting for transfers between devices, body(): lax.psum_scatter(local_grad, 'dp', scatter_dimension=0, tiled=True)  46 us
    all_to_all x1, starting transfers between devices, body(): lax.all_to_all(request_len, 'table', split_axis=0, concat_axis=0, tiled=T...  19.3 us
    gather x1, local copies, waits for them, and re-layouts, body(): looked_up = jnp.where(live_mask[..., None], updated[asked_rows], 0.0)  19.1 us
    another operation x3, other arithmetic  19 us
    scatter x2, local copies, waits for them, and re-layouts, body(): request_rows = jnp.zeros((peers * capacity, slot_count), jnp.int32).at[po...  17.5 us
  transfers between devices with their start and end apart: 7, of which 4 were waited for; matrix products, arithmetic and copies ran while one was open for 7% of the time, Pallas kernels for 0%

commit v1 on v0

v1 whole, which is shorter than its diff:
```python
import functools
import jax
import jax.numpy as jnp
from jax import lax
from jax.experimental import pallas as pl
from jax.experimental.pallas import tpu as pltpu
from jax.sharding import PartitionSpec as P

loss_scale = 64.0
SLOTS = 80
LANES = 128
VM = pltpu.VMEM
NT = (((1,), (1,)), ((), ()))


def vspec():
    return pl.BlockSpec(memory_space=pltpu.VMEM)


def request_kernel(own_ref, row_ref, len_ref, req_ref, pos_ref, acc_ref):
    features, samples = own_ref.shape
    peers = req_ref.shape[0]
    dead = jnp.int32(2048)
    up = lax.broadcasted_iota(jnp.int32, (samples, samples), 0) < lax.broadcasted_iota(
        jnp.int32, (samples, samples), 1
    )
    before = jnp.where(up, 1.0, 0.0).astype(jnp.bfloat16)
    ones = jnp.ones((samples, samples), jnp.bfloat16)
    holder = lax.broadcasted_iota(jnp.int32, (peers, samples), 0)
    slot = lax.broadcasted_iota(jnp.int32, (SLOTS, samples), 0).astype(jnp.float32)
    acc_ref[...] = jnp.zeros_like(acc_ref)

    def step(f, carry):
        own = own_ref[pl.ds(f, 1), :]
        hit = own == holder
        onehot = jnp.where(hit, 1.0, 0.0)
        narrow = onehot.astype(jnp.bfloat16)
        prior = jnp.dot(narrow, before, preferred_element_type=jnp.float32) + carry
        rank = jnp.sum(onehot * prior, axis=0, keepdims=True)
        carry = carry + jnp.dot(narrow, ones, preferred_element_type=jnp.float32)
        pos_ref[pl.ds(f, 1), :] = own * SLOTS + rank.astype(jnp.int32)
        rows = row_ref[f]
        first = rows[0:1, :]
        second = jnp.where(len_ref[pl.ds(f, 1), :] > 1, rows[1:2, :], dead)
        at = slot == rank
        pieces = []
        for value in (first, second):
            for part in (value // 128, value % 128):
                pieces.append(jnp.where(at, part.astype(jnp.float32), 0.0))
        placed = jnp.concatenate(pieces, axis=0).astype(jnp.bfloat16)
        mark = jnp.where(at, 1.0, 0.0).astype(jnp.bfloat16)
        placed = jnp.concatenate([placed, mark], axis=0)
        acc_ref[...] += lax.dot_general(narrow, placed, NT, preferred_element_type=jnp.float32)
        return carry

    lax.fori_loop(0, features, step, jnp.zeros((peers, samples), jnp.float32))
    acc = acc_ref[...]
    filled = acc[:, 4 * SLOTS : 5 * SLOTS] > 0.5
    for q in range(2):
        high = acc[:, 2 * q * SLOTS : (2 * q + 1) * SLOTS]
        low = acc[:, (2 * q + 1) * SLOTS : (2 * q + 2) * SLOTS]
        ids = jnp.where(filled, (high * 128.0 + low).astype(jnp.int32), dead)
        req_ref[:, q, :] = ids


def build_requests(own, rows, lens, peers):
    features, samples = own.shape
    return pl.pallas_call(
        request_kernel,
        out_shape=(
            jax.ShapeDtypeStruct((peers, 2, SLOTS), jnp.int32),
            jax.ShapeDtypeStruct((features, samples), jnp.int32),
        ),
        in_specs=[vspec()] * 3,
        out_specs=(vspec(), vspec()),
        scratch_shapes=[VM((peers, 5 * SLOTS), jnp.float32)],
        name="requests",
    )(own, rows, lens)


def update_kernel(ver_ref, loc_ref, cver_ref, table_ref, conf_ref, out_ref, work_ref):
    work_ref[...] = table_ref[...]

    def step(block, carry):
        for u in range(8):
            i = block * 8 + u
            g = loc_ref[i]

            @pl.when(cver_ref[i] > ver_ref[g])
            def _():
                work_ref[pl.ds(g, 1), :] = conf_ref[pl.ds(i, 1), :]

        return carry

    lax.fori_loop(0, conf_ref.shape[0] // 8, step, 0)
    now = work_ref[...]
    high = now.astype(jnp.bfloat16)
    out_ref[:, 0:LANES] = high
    out_ref[:, LANES : 2 * LANES] = (now - high.astype(jnp.float32)).astype(jnp.bfloat16)


def update_table(versions, conf_local, conf_version, table, conf_values):
    smem = pl.BlockSpec(memory_space=pltpu.SMEM)
    return pl.pallas_call(
        update_kernel,
        out_shape=jax.ShapeDtypeStruct((table.shape[0], 2 * LANES), jnp.bfloat16),
        in_specs=[smem, smem, smem, vspec(), vspec()],
        out_specs=vspec(),
        scratch_shapes=[VM(table.shape, jnp.float32)],
        name="update",
    )(versions, conf_local, conf_version, table, conf_values)


GROUP = 8


def lookup_kernel(req_ref, table_ref, out_ref, hot_ref):
    blocks = table_ref.shape[0] // LANES
    lane = lax.broadcasted_iota(jnp.int32, (SLOTS, LANES), 1)
    zero = jnp.zeros((SLOTS, LANES), jnp.bfloat16)
    columns = [jnp.transpose(req_ref[:, q, :]) for q in range(2)]
    for u in range(GROUP):
        low, high = [], []
        for q in range(2):
            ids = jnp.broadcast_to(columns[q][:, u : u + 1], (SLOTS, LANES))
            low.append(jnp.where((ids & 127) == lane, 1.0, 0.0).astype(jnp.bfloat16))
            high.append((ids >> 7).astype(jnp.float32).astype(jnp.bfloat16))
        for k in range(blocks):
            k16 = jnp.bfloat16(k)
            hot = jnp.where(high[0] == k16, low[0], zero) + jnp.where(high[1] == k16, low[1], zero)
            hot_ref[u * SLOTS : (u + 1) * SLOTS, k * LANES : (k + 1) * LANES] = hot
    both = jnp.dot(hot_ref[...], table_ref[...], preferred_element_type=jnp.float32)
    out_ref[...] = (both[:, :LANES] + both[:, LANES:]).astype(jnp.bfloat16)


def lookup(req, table):
    peers = req.shape[0]
    rows = table.shape[0]
    return pl.pallas_call(
        lookup_kernel,
        out_shape=jax.ShapeDtypeStruct((peers * SLOTS, LANES), jnp.bfloat16),
        grid=(peers // GROUP,),
        in_specs=[
            pl.BlockSpec((GROUP, 2, SLOTS), lambda g: (g, 0, 0)),
            pl.BlockSpec((rows, 2 * LANES), lambda g: (0, 0)),
        ],
        out_specs=pl.BlockSpec((GROUP * SLOTS, LANES), lambda g: (g, 0)),
        scratch_shapes=[VM((GROUP * SLOTS, rows), jnp.bfloat16)],
        name="lookup",
    )(req, table)


def scatter_kernel(ids_ref, grad_ref, out_ref, hot_ref):
    rows = out_ref.shape[0]
    blocks = rows // LANES
    line = lax.broadcasted_iota(jnp.int32, (LANES, LANES), 0)
    zero = jnp.zeros((LANES, LANES), jnp.bfloat16)
    per = GROUP * SLOTS // LANES

    @pl.when(pl.program_id(0) == 0)
    def _():
        out_ref[...] = jnp.zeros_like(out_ref)

    for c in range(per):
        low, high = [], []
        for q in range(2):
            ids = ids_ref[0, q, c : c + 1, :]
            low.append(jnp.where((ids & 127) == line, 1.0, 0.0).astype(jnp.bfloat16))
            wide = jnp.broadcast_to((ids >> 7).astype(jnp.float32), (LANES, LANES))
            high.append(wide.astype(jnp.bfloat16))
        for k in range(blocks):
            k16 = jnp.bfloat16(k)
            hot = jnp.where(high[0] == k16, low[0], zero) + jnp.where(high[1] == k16, low[1], zero)
            hot_ref[k * LANES : (k + 1) * LANES, c * LANES : (c + 1) * LANES] = hot
    out_ref[...] += jnp.dot(hot_ref[...], grad_ref[...], preferred_element_type=jnp.float32)


def scatter_add(ids, grad, rows):
    groups, _, per, _ = ids.shape
    return pl.pallas_call(
        scatter_kernel,
        out_shape=jax.ShapeDtypeStruct((rows, LANES), jnp.float32),
        grid=(groups,),
        in_specs=[
            pl.BlockSpec((1, 2, per, LANES), lambda g: (g, 0, 0, 0)),
            pl.BlockSpec((GROUP * SLOTS, LANES), lambda g: (g, 0)),
        ],
        out_specs=pl.BlockSpec((rows, LANES), lambda g: (0, 0)),
        scratch_shapes=[VM((rows, GROUP * SLOTS), jnp.bfloat16)],
        name="scatter",
    )(ids, grad)


def middle_kernel(
    pos_ref, ans_ref, dense_ref, label_ref, bias_ref, head_ref, down_hbm, up_hbm,
    logit_ref, send_ref,
    rows_ref, base_ref, factor_ref, back_ref, down_ref, up_ref, sems,
):
    samples = dense_ref.shape[0]
    features = pos_ref.shape[0]
    width = base_ref.shape[2]
    loads = [
        pltpu.make_async_copy(down_hbm, down_ref, sems.at[0]),
        pltpu.make_async_copy(up_hbm, up_ref, sems.at[1]),
    ]
    for load in loads:
        load.start()
    rows_ref[...] = ans_ref[...].astype(jnp.float32)
    base_ref[:, :, 0:LANES] = dense_ref[...].astype(jnp.float32).reshape(samples // 8, 8, LANES)

    def fetch(block, carry):
        b0 = block * 8
        for f in range(features):
            for u in range(8):
                row = rows_ref[pl.ds(pos_ref[f, b0 + u], 1), :]
                base_ref[block, u : u + 1, (f + 1) * LANES : (f + 2) * LANES] = row
        return carry

    lax.fori_loop(0, samples // 8, fetch, 0)
    inputs = base_ref[...].reshape(samples, width).astype(jnp.bfloat16)
    loads[0].wait()
    crossed = lax.dot_general(inputs, down_ref[...], NT, preferred_element_type=jnp.float32)
    crossed = crossed.astype(jnp.bfloat16)
    loads[1].wait()
    base = inputs.astype(jnp.float32)
    head = head_ref[...]
    factor = jnp.dot(crossed, up_ref[...], preferred_element_type=jnp.float32) + bias_ref[...]
    factor_ref[...] = factor
    logits = jnp.sum((base * factor + base) * head, axis=1, keepdims=True)
    logit_ref[...] = logits
    signal = loss_scale * (jax.nn.sigmoid(logits) - label_ref[...].astype(jnp.float32))
    lift = (signal * head * base).astype(jnp.bfloat16)
    cross = lax.dot_general(lift, up_ref[...], NT, preferred_element_type=jnp.float32)
    cross = cross.astype(jnp.bfloat16)
    state = signal * head
    back = (
        state
        + jnp.dot(cross, down_ref[...], preferred_element_type=jnp.float32)
        + state * factor_ref[...]
    )
    back_ref[...] = back.reshape(samples // 8, 8, width)
    rows_ref[...] = jnp.zeros_like(rows_ref)

    def place(block, carry):
        b0 = block * 8
        for f in range(features):
            for u in range(8):
                row = back_ref[block, u : u + 1, (f + 1) * LANES : (f + 2) * LANES]
                rows_ref[pl.ds(pos_ref[f, b0 + u], 1), :] = row
        return carry

    lax.fori_loop(0, samples // 8, place, 0)
    send_ref[...] = rows_ref[...].astype(jnp.bfloat16)


def middle(pos, answer, dense_out, labels, bias, head, down, up):
    samples = dense_out.shape[0]
    rank, width = down.shape
    total = answer.shape[0]
    smem = pl.BlockSpec(memory_space=pltpu.SMEM)
    hbm = pl.BlockSpec(memory_space=pl.ANY)
    return pl.pallas_call(
        middle_kernel,
        out_shape=(
            jax.ShapeDtypeStruct((samples, 1), jnp.float32),
            jax.ShapeDtypeStruct((total, LANES), jnp.bfloat16),
        ),
        in_specs=[smem, vspec(), vspec(), vspec(), vspec(), vspec(), hbm, hbm],
        out_specs=(vspec(), vspec()),
        scratch_shapes=[
            VM((total, LANES), jnp.float32),
            VM((samples // 8, 8, width), jnp.float32),
            VM((samples, width), jnp.float32),
            VM((samples // 8, 8, width), jnp.float32),
            VM((rank, width), jnp.bfloat16),
            VM((rank, width), jnp.bfloat16),
            pltpu.SemaphoreType.DMA((2,)),
        ],
        compiler_params=pltpu.CompilerParams(vmem_limit_bytes=40 << 20),
        name="middle",
    )(pos, answer, dense_out, labels, bias, head, down, up)


def body(
    emb_table, versions, conf_local, conf_version, conf_values, owners, row_local, lengths,
    dense_out, labels, cross_down, cross_up, cross_bias, head_weight,
):
    peers = lax.axis_size("table")
    copies = lax.axis_size("dp")
    rows_dev, emb_width = emb_table.shape
    samples, features, slot_count = row_local.shape
    own = owners.reshape(samples, features).T
    rows = jnp.transpose(row_local, (1, 2, 0))
    req, pos = build_requests(own, rows, lengths.T, peers)
    down_local = cross_down[0].T
    down = lax.all_gather(down_local, "dp", axis=0, tiled=True)
    up = lax.all_gather(cross_up[0], "dp", axis=0, tiled=True)
    asked = lax.all_to_all(req, "table", split_axis=0, concat_axis=0, tiled=True)
    table = update_table(versions, conf_local, conf_version, emb_table, conf_values)
    found = lookup(asked, table).reshape(peers, SLOTS, emb_width)
    answer = lax.all_to_all(found, "table", split_axis=0, concat_axis=0, tiled=True)
    flat = asked.reshape(peers // GROUP, GROUP, 2, SLOTS).transpose(0, 2, 1, 3)
    flat = flat.reshape(peers // GROUP, 2, GROUP * SLOTS // LANES, LANES)
    logits, send = middle(
        pos,
        answer.reshape(peers * SLOTS, emb_width),
        dense_out,
        labels.reshape(samples, 1),
        cross_bias,
        head_weight.reshape(1, -1),
        down,
        up,
    )
    got = lax.all_to_all(
        send.reshape(peers, SLOTS, emb_width), "table", split_axis=0, concat_axis=0, tiled=True
    )
    local = scatter_add(flat, got.reshape(peers * SLOTS, emb_width), rows_dev)
    emb_grad = lax.psum_scatter(local, "dp", scatter_dimension=0, tiled=True)
    return (logits.reshape(samples), emb_grad)


def solution(mesh):
    in_specs = (
        P("table", None),
        P("table"),
        P("table"),
        P("table"),
        P("table", None),
        P(("table", "dp"), None, None),
        P(("table", "dp"), None, None),
        P(("table", "dp"), None),
        P(("table", "dp"), None),
        P(("table", "dp")),
        P(None, None, "dp"),
        P(None, "dp", None),
        P(),
        P(),
    )
    out_specs = (P(("table", "dp")), P(("table", "dp"), None))
    return jax.shard_map(body, mesh=mesh, in_specs=in_specs, out_specs=out_specs, check_vma=False)
```

time: 678 us -> 281 us (0.41)
  waiting for transfers between devices: 392 us -> 165 us
  other arithmetic: 111 us -> 0.63 us
  local copies, waits for them, and re-layouts: 95.8 us -> 7.89 us
  Pallas kernels: 0 us -> 54.8 us
  starting transfers between devices: 51.7 us -> 37.4 us
  matrix products: 12.8 us -> 0 us
    all_to_all x4 -> x3, waiting for transfers between devices: 344 us -> 128 us  [the longest x1 60.5 us: body(): lax.all_to_all(found, 'table', split_axis=0, concat_axis=0, tiled=True)]
    scatter-add x1 -> x0, other arithmetic: 63.2 us -> none  [body(): local_grad = jnp.zeros((rows_dev, emb_width), jnp.float32).at[got_rows.re...]
    pallas_call x0 -> x5, Pallas kernels: none -> 54.8 us  [the longest x1 15.8 us: middle(): pl.pallas_call(middle_kernel, out_shape=(jax.ShapeDtypeStruct((samples, 1...]
    scatter x4 -> x0, local copies, waits for them, and re-layouts: 44.3 us -> none  [the longest x2 17.5 us: body(): request_rows = jnp.zeros((peers * capacity, slot_count), jnp.int32).at[po...]
    gather x3 -> x0, local copies, waits for them, and re-layouts: 27.4 us -> none  [the longest x1 19.1 us: body(): looked_up = jnp.where(live_mask[..., None], updated[asked_rows], 0.0)]
    another operation x3 -> x0, other arithmetic: 19 us -> none
    all_to_all x4 -> x3, starting transfers between devices: 51.3 us -> 37.2 us  [the longest x1 19.3 us: body(): lax.all_to_all(req, 'table', split_axis=0, concat_axis=0, tiled=True)]
    dot_general x2 -> x0, matrix products: 12.8 us -> none  [the longest x1 7.43 us: dense_step(): jnp.dot(crossed, cross_up[cross_index], preferred_element_type=jnp.float32)]
  transfers between devices with their start and end apart: 7 -> 6, of which waited for: 4 -> 4; matrix products, arithmetic and copies ran while one was open for 7% -> 1% of each run, Pallas kernels for 0% -> 11%
where the time goes in v1:
time: 281 us; the launch traced here: 279 us
  waiting for transfers between devices  165 us (59%)
  Pallas kernels  54.8 us (20%)
  starting transfers between devices  37.4 us (13%)
  between operations  13.9 us (5%)
  local copies, waits for them, and re-layouts  7.89 us (3%)
    all_to_all x1, waiting for transfers between devices, body(): lax.all_to_all(found, 'table', split_axis=0, concat_axis=0, tiled=True)  60.5 us
    all_to_all x1, waiting for transfers between devices, body(): lax.all_to_all(send.reshape(peers, SLOTS, emb_width), 'table', split_axis...  59.8 us
    reduce_scatter x1, waiting for transfers between devices, body(): emb_grad = lax.psum_scatter(local, 'dp', scatter_dimension=0, tiled=True)  35.2 us
    all_to_all x1, starting transfers between devices, body(): lax.all_to_all(req, 'table', split_axis=0, concat_axis=0, tiled=True)  19.3 us
    pallas_call x1, Pallas kernels, middle(): pl.pallas_call(middle_kernel, out_shape=(jax.ShapeDtypeStruct((samples, 1...  15.8 us
    pallas_call x1, Pallas kernels, lookup(): pl.pallas_call(lookup_kernel, out_shape=jax.ShapeDtypeStruct((peers * SLO...  13.6 us
    all_to_all x1, starting transfers between devices, body(): lax.all_to_all(send.reshape(peers, SLOTS, emb_width), 'table', split_axis...  11.1 us
    pallas_call x1, Pallas kernels, build_requests(): pl.pallas_call(request_kernel, out_shape=(jax.ShapeDtypeStruct((peers, 2,...  10.3 us
  transfers between devices with their start and end apart: 6, of which 4 were waited for; matrix products, arithmetic and copies ran while one was open for 1% of the time, Pallas kernels for 11%

profile of v1, /device:TPU:1, one launch (start us, length us, event | category | flops | bytes accessed | tf_op | source)
XLA Modules:
  0.0 279.3 jit_solution(4841752007312621766)
XLA Ops:
  7.2 0.0 all-gather.4.cloned.1.call-start
  7.2 0.7 all-gather.4.cloned.1.call-update
  7.9 0.0 all-gather.6.cloned.1.call-start
  7.9 0.7 all-gather.6.cloned.1.call-update
  8.6 1.3 copy.24
  10.0 10.3 %requests.1 = (s32[64,2,80]{2,1,0:T(2,128)}, s32[26,128]{1,0:T(8,128)}) custom-call(s32[26,128]{1,0:T(8,128)} %bitcast.29, s32[26,2,128]{2,1,0:T(2,128)} %bitcast.30, s32[26,128]{1,0:T(8,128)} %bitcast.31), custom_call_target="tpu_custom_call" | custom-call | tf_op jit(solution)/shard_map/requests/pallas_call | solution.py:68
  20.3 19.3 %all-to-all-start = ((s32[64,2,80]{2,1,0:T(2,128)}), s32[64,2,80]{2,1,0:T(2,128)S(1)}, u32[]{:S(2)}, u32[]{:S(2)}) async-start(s32[64,2,80]{2,1,0:T(2,128)} %get-tuple-element.7), calls=%async_computation | async-start | bytes 131072 | tf_op jit(solution)/shard_map/all_to_all | solution.py:298
  39.6 5.6 %update.1.table_ref = bf16[2048,256]{1,0:T(8,128)(2,1)} custom-call(s32[2048]{0:T(1024)} %ver_ref.1, s32[256]{0:T(256)} %loc_ref.1, s32[256]{0:T(256)} %cver_ref.1, f32[2048,128]{1,0:T(8,128)} %table_ref.1, f32[256,128]{1,0:T(8,128)} %conf_ref.1), custom_call_target="tpu_custom_call" | custom-call | tf_op jit(solution)/shard_map/update/pallas_call | solution.py:104
  45.2 7.9 %all-to-all-done.req_ref = s32[64,2,80]{2,1,0:T(2,128)S(1)} async-done(((s32[64,2,80]{2,1,0:T(2,128)}), s32[64,2,80]{2,1,0:T(2,128)S(1)}, u32[]{:S(2)}, u32[]{:S(2)}) %all-to-all-start) | async-done | bytes 40992 | tf_op jit(solution)/shard_map/all_to_all | solution.py:298
  53.1 0.0 copy-start.6
  53.1 0.6 copy-done.6
  53.7 13.6 %lookup.1 = bf16[5120,128]{1,0:T(8,128)(2,1)} custom-call(s32[64,2,80]{2,1,0:T(2,128)} %copy-done.6, bf16[2048,256]{1,0:T(8,128)(2,1)} %update.1.table_ref), custom_call_target="tpu_custom_call" | custom-call | tf_op jit(solution)/shard_map/lookup/pallas_call | solution.py:139
  67.3 0.0 copy-start.8
  67.3 0.0 copy-start.9
  67.3 0.0 copy-start.2
  67.3 0.0 copy-start.3
  67.3 0.0 copy-start.4
  67.4 6.8 %all-to-all-start.1 = ((bf16[64,80,128]{2,1,0:T(8,128)(2,1)}), bf16[64,80,128]{2,1,0:T(8,128)(2,1)S(1)}, u32[]{:S(2)}, u32[]{:S(2)}) async-start(bf16[64,80,128]{2,1,0:T(8,128)(2,1)} %bitcast.25), calls=%async_computation.1 | async-start | bytes 2621440 | tf_op jit(solution)/shard_map/all_to_all | solution.py:301
  74.2 0.0 copy-done.8
  74.2 0.0 copy-done.9
  74.2 0.1 copy.18.label_ref
  74.3 60.5 %all-to-all-done.1 = bf16[64,80,128]{2,1,0:T(8,128)(2,1)S(1)} async-done(((bf16[64,80,128]{2,1,0:T(8,128)(2,1)}), bf16[64,80,128]{2,1,0:T(8,128)(2,1)S(1)}, u32[]{:S(2)}, u32[]{:S(2)}) %all-to-all-start.1) | async-done | bytes 1310752 | tf_op jit(solution)/shard_map/all_to_all | solution.py:301
  134.8 0.0 all-gather.4.cloned.1.call-done.down_hbm
  134.8 0.0 all-gather.6.cloned.1.call-done
  134.8 0.0 copy-done.2
  134.8 0.0 copy-done.3
  134.8 0.0 copy-done.4
  134.8 0.0 copy-start
  134.8 2.0 copy-done
  136.8 0.0 copy-start.1
  136.8 2.0 copy-done.1
  138.8 15.8 %middle.1 = (f32[128,1]{1,0:T(8,128)S(1)}, bf16[5120,128]{1,0:T(8,128)(2,1)}) custom-call(s32[26,128]{1,0:T(8,128)S(1)} %copy-done.3, bf16[5120,128]{1,0:T(8,128)(2,1)S(1)} %bitcast.22, bf16[128,128]{1,0:T(8,128)(2,1)S(1)} %copy-done.2, s32[128,1]{1,0:T(8,128)S(1)} %copy.18.label_ref, f32[1,3456]{1,0:T(1,128)S(1)} %copy-done.4, ...), custom_call_target="tpu_custom_call" | custom-call | tf_op jit(solution)/shard_map/middle/pallas_call | solution.py:262
  154.7 0.0 copy-start.7
  154.7 11.1 %all-to-all-start.2 = ((bf16[64,80,128]{2,1,0:T(8,128)(2,1)}), bf16[64,80,128]{2,1,0:T(8,128)(2,1)S(1)}, u32[]{:S(2)}, u32[]{:S(2)}) async-start(bf16[64,80,128]{2,1,0:T(8,128)(2,1)} %bitcast.11), calls=%async_computation.2 | async-start | bytes 2621440 | tf_op jit(solution)/shard_map/all_to_all | solution.py:314
  165.9 0.0 reduce-scatter.2.cloned.1.call-start
  165.9 0.0 copy-done.7
  165.9 0.7 reshape.41.ids_ref
  166.6 59.8 %all-to-all-done.2 = bf16[64,80,128]{2,1,0:T(8,128)(2,1)S(1)} async-done(((bf16[64,80,128]{2,1,0:T(8,128)(2,1)}), bf16[64,80,128]{2,1,0:T(8,128)(2,1)S(1)}, u32[]{:S(2)}, u32[]{:S(2)}) %all-to-all-start.2) | async-done | bytes 1310752 | tf_op jit(solution)/shard_map/all_to_all | solution.py:314
  226.5 0.0 copy-start.5
  226.5 1.1 copy-done.5
  227.5 9.4 %scatter.1 = f32[2048,128]{1,0:T(8,128)} custom-call(s32[8,2,5,128]{3,2,1,0:T(8,128)} %reshape.41.ids_ref, bf16[5120,128]{1,0:T(8,128)(2,1)} %bitcast.24), custom_call_target="tpu_custom_call" | custom-call | tf_op jit(solution)/shard_map/scatter/pallas_call | solution.py:180
  236.9 0.0 reduce-scatter.2.cloned.1.call-update
  236.9 0.6 reduce
  237.6 35.2 %reduce-scatter.2.cloned.1.call-done = f32[256,128]{1,0:T(8,128)} async-done(((f32[2048,128]{1,0:T(8,128)}), f32[256,128]{1,0:T(8,128)}) %reduce-scatter.2.cloned.1.call-update) | async-done | bytes 131088 | tf_op jit(solution)/shard_map/reduce_scatter | solution.py:318
  (2 shorter events, 0.0 us)
Async XLA Ops:
  7.2 127.7 %all-gather.4.cloned.1.call-start = ((), (), s32[]{:S(2)}) async-start(), calls=%async_computation.4 | async-start | bytes 3981312 | tf_op jit(solution)/shard_map/all_gather | solution.py:296
  7.9 126.9 %all-gather.6.cloned.1.call-start = ((), (), s32[]{:S(2)}) async-start(), calls=%async_computation.6 | async-start | bytes 3981312 | tf_op jit(solution)/shard_map/all_gather | solution.py:297
  20.3 32.8 %all-to-all-start = ((s32[64,2,80]{2,1,0:T(2,128)}), s32[64,2,80]{2,1,0:T(2,128)S(1)}, u32[]{:S(2)}, u32[]{:S(2)}) async-start(s32[64,2,80]{2,1,0:T(2,128)} %get-tuple-element.7), calls=%async_computation | async-start | bytes 131072 | tf_op jit(solution)/shard_map/all_to_all | solution.py:298
  53.1 0.6 copy-start.6
  67.3 6.9 %copy-start.8 = (f32[3456]{0:T(1024)S(1)}, f32[3456]{0:T(1024)}, u32[]{:S(2)}) copy-start(f32[3456]{0:T(1024)} %param.27) | copy-start | bytes 41476
  67.3 6.9 %copy-start.9 = (s32[128]{0:T(128)S(1)}, s32[128]{0:T(128)}, u32[]{:S(2)}) copy-start(s32[128]{0:T(128)} %param.23) | copy-start | bytes 1540
  67.3 67.5 %copy-start.2 = (bf16[128,128]{1,0:T(8,128)(2,1)S(1)}, bf16[128,128]{1,0:T(8,128)(2,1)}, u32[]{:S(2)}) copy-start(bf16[128,128]{1,0:T(8,128)(2,1)} %dense_ref.1) | copy-start | bytes 98308
  67.3 67.5 %copy-start.3 = (s32[26,128]{1,0:T(8,128)S(1)}, s32[26,128]{1,0:T(8,128)}, u32[]{:S(2)}) copy-start(s32[26,128]{1,0:T(8,128)} %get-tuple-element.6.pos_ref) | copy-start | bytes 39940
  67.3 67.5 %copy-start.4 = (f32[1,3456]{1,0:T(1,128)S(1)}, f32[1,3456]{1,0:T(1,128)}, u32[]{:S(2)}) copy-start(f32[1,3456]{1,0:T(1,128)} %bias_ref.1) | copy-start | bytes 41476
  67.4 67.5 %all-to-all-start.1 = ((bf16[64,80,128]{2,1,0:T(8,128)(2,1)}), bf16[64,80,128]{2,1,0:T(8,128)(2,1)S(1)}, u32[]{:S(2)}, u32[]{:S(2)}) async-start(bf16[64,80,128]{2,1,0:T(8,128)(2,1)} %bitcast.25), calls=%async_computation.1 | async-start | bytes 2621440 | tf_op jit(solution)/shard_map/all_to_all | solution.py:301
  134.8 2.0 copy-start
  136.8 2.0 copy-start.1
  154.7 11.2 %copy-start.7 = (s32[64,2,80]{2,1,0:T(2,128)S(1)}, s32[64,2,80]{2,1,0:T(2,128)}, u32[]{:S(2)}) copy-start(s32[64,2,80]{2,1,0:T(2,128)} %copy-done.6) | copy-start | bytes 122884
  154.7 71.8 %all-to-all-start.2 = ((bf16[64,80,128]{2,1,0:T(8,128)(2,1)}), bf16[64,80,128]{2,1,0:T(8,128)(2,1)S(1)}, u32[]{:S(2)}, u32[]{:S(2)}) async-start(bf16[64,80,128]{2,1,0:T(8,128)(2,1)} %bitcast.11), calls=%async_computation.2 | async-start | bytes 2621440 | tf_op jit(solution)/shard_map/all_to_all | solution.py:314
  165.9 106.9 %reduce-scatter.2.cloned.1.call-start = ((), (), s32[]{:S(2)}) async-start(), calls=%async_computation.5 | async-start | bytes 1179648 | tf_op jit(solution)/shard_map/reduce_scatter | solution.py:318
  226.5 1.1 copy-start.5
Sparse Core Ops, SparseCore 0:
  10.1 42.6 all-gather.3
  55.0 36.9 all-gather.5
  237.1 35.6 reduce-scatter.1

commit v2 on v0

v2 whole, which is shorter than its diff:
```python
import jax
import jax.numpy as jnp
from jax import lax
from jax.experimental import pallas as pl
from jax.experimental.pallas import tpu as pltpu
from jax.sharding import PartitionSpec as P

loss_scale = 64.0
PEERS = 64
COPIES = 8
RING_Y = 4
RING_Z = 16
SLOTS = 80
LANES = 128
GROUP = 8
DEAD = 2048
PARTS = 7
VM = pltpu.VMEM
MESH = pl.DeviceIdType.MESH
NT = (((1,), (1,)), ((), ()))
BF = jnp.bfloat16
F32 = jnp.float32


def offset_of(j):
    t = j % RING_Z
    half = (t + 1) // 2
    odd = t % 2
    return j // RING_Z, odd * half + (1 - odd) * (RING_Z - half)


def shifted(j, here, sign):
    dy, dz = offset_of(j)
    y = (here // RING_Z + RING_Y + sign * dy) % RING_Y
    z = (here % RING_Z + 2 * RING_Z + sign * dz) % RING_Z
    return y * RING_Z + z


def slot_of_owner(own, here):
    dy = (own // RING_Z - here // RING_Z + RING_Y) & (RING_Y - 1)
    dz = (own % RING_Z - here % RING_Z + RING_Z) & (RING_Z - 1)
    t = jnp.where(dz == 0, 0, jnp.where(dz <= RING_Z // 2, 2 * dz - 1, 2 * (RING_Z - dz)))
    return dy * RING_Z + t


def step_kernel(
    own_ref, row_ref, len_ref, ver_ref, loc_ref, cver_ref, table_ref, conf_ref,
    dense_ref, label_ref, downl_ref, upl_ref, bias_ref, head_ref,
    logit_ref, out_ref,
    hits_ref, prior_ref, wide_ref, placed_ref, req_ref, asked_ref, pos_v, inv_v, pos_s, inv_s,
    tab_ref, hot_ref, found_ref, ans_ref, rows_ref, base_ref, factor_ref, back_ref,
    down_ref, up_ref, stage_ref, gsend_ref, grecv_ref, hot2_ref, acc_ref, rsend_ref, rrecv_ref,
    q_send, q_recv, a_send, a_recv, g_send, g_recv, w_send, w_recv, c_send, c_recv, r_send, r_recv,
    l_sem,
):
    table_at = lax.axis_index("table")
    dp_at = lax.axis_index("dp")
    features, samples = own_ref.shape
    total = PEERS * SLOTS
    width = bias_ref.shape[1]
    shard = downl_ref.shape[0]
    blocks = table_ref.shape[0] // LANES

    barrier = pltpu.get_barrier_semaphore()

    def greet(j, carry):
        pl.semaphore_signal(
            barrier, inc=1, device_id=(shifted(j, table_at, 1), dp_at), device_id_type=MESH
        )
        return carry

    lax.fori_loop(1, PEERS, greet, 0)
    for k in range(1, COPIES):
        pl.semaphore_signal(
            barrier, inc=1, device_id=(table_at, (dp_at + k) % COPIES), device_id_type=MESH
        )

    grecv_ref[:, SLOTS:LANES, :] = jnp.zeros((PEERS, LANES - SLOTS, LANES), BF)
    acc_ref[...] = jnp.zeros_like(acc_ref)

    holder = lax.broadcasted_iota(jnp.int32, (PEERS, samples), 0)

    def mark_hits(f, carry):
        hit = jnp.where(slot_of_owner(own_ref[pl.ds(f, 1), :], table_at) == holder, 1.0, 0.0)
        hit = hit.astype(BF)
        hits_ref[pl.ds(pl.multiple_of(f * PEERS, PEERS), PEERS), :] = hit
        wide_ref[:, pl.ds(pl.multiple_of(f * LANES, LANES), LANES)] = hit
        return carry

    lax.fori_loop(0, features, mark_hits, 0)
    row_at = lax.broadcasted_iota(jnp.int32, (samples, 2 * samples), 0)
    col_at = lax.broadcasted_iota(jnp.int32, (samples, 2 * samples), 1)
    before = jnp.where((row_at < col_at) | (col_at >= samples), 1.0, 0.0).astype(BF)
    prior_ref[...] = jnp.dot(hits_ref[...], before, preferred_element_type=F32)
    slot = lax.broadcasted_iota(jnp.int32, (SLOTS, samples), 0).astype(F32)
    sample = lax.broadcasted_iota(jnp.int32, (1, samples), 1).astype(F32)

    def rank_bags(f, carry):
        at = pl.ds(pl.multiple_of(f * PEERS, PEERS), PEERS)
        onehot = hits_ref[at, :].astype(F32)
        rank = jnp.sum(onehot * (prior_ref[at, 0:samples] + carry), axis=0, keepdims=True)
        owner = slot_of_owner(own_ref[pl.ds(f, 1), :], table_at)
        pos_v[pl.ds(f, 1), :] = owner * SLOTS + jnp.clip(rank.astype(jnp.int32), 0, SLOTS - 1)
        both = row_ref[f]
        first = both[0:1, :]
        second = jnp.where(len_ref[pl.ds(f, 1), :] > 1, both[1:2, :], DEAD)
        here = slot == rank
        lanes = pl.ds(pl.multiple_of(f * LANES, LANES), LANES)
        values = []
        for value in (first, second):
            values.append((value >> 7).astype(F32))
            values.append((value & 127).astype(F32))
        values.append(jnp.broadcast_to(f.astype(F32), (1, samples)))
        values.append(sample)
        values.append(jnp.ones((1, samples), F32))
        for p, value in enumerate(values):
            placed = jnp.where(here, value, 0.0).astype(BF)
            placed_ref[p * SLOTS : (p + 1) * SLOTS, lanes] = placed
        return carry + prior_ref[at, samples : 2 * samples]

    lax.fori_loop(0, features, rank_bags, jnp.zeros((PEERS, samples), F32))
    packed = lax.dot_general(wide_ref[...], placed_ref[...], NT, preferred_element_type=F32)
    part = [packed[:, p * SLOTS : (p + 1) * SLOTS] for p in range(PARTS)]
    filled = part[6] > 0.5
    dead_tail = jnp.full((PEERS, LANES - SLOTS), DEAD, jnp.int32)
    for q in range(2):
        ids = (part[2 * q] * 128.0 + part[2 * q + 1]).astype(jnp.int32)
        ids = jnp.where(filled, ids, DEAD)
        req_ref[:, q, :] = jnp.concatenate([ids, dead_tail], axis=1)
    inverse = (part[4] * 128.0 + part[5]).astype(jnp.int32)
    inverse = jnp.clip(inverse, 0, features * samples - 1)
    inv_v[...] = jnp.concatenate([inverse, jnp.zeros_like(dead_tail)], axis=1)

    to_smem = [
        pltpu.make_async_copy(pos_v, pos_s, l_sem.at[0]),
        pltpu.make_async_copy(inv_v, inv_s, l_sem.at[1]),
    ]
    for copy in to_smem:
        copy.start()
    own_request = pltpu.make_async_copy(req_ref.at[0], asked_ref.at[0], l_sem.at[2])
    own_request.start()

    pl.semaphore_wait(barrier, PEERS - 1 + COPIES - 1)

    def request_copy(j):
        return pltpu.make_async_remote_copy(
            src_ref=req_ref.at[j], dst_ref=asked_ref.at[j],
            send_sem=q_send.at[j], recv_sem=q_recv.at[j],
            device_id=(shifted(j, table_at, 1), dp_at), device_id_type=MESH,
        )

    def send_request(j, carry):
        request_copy(j).start()
        return carry

    lax.fori_loop(1, PEERS, send_request, 0)

    core, chip = dp_at % 2, dp_at // 2
    chips = COPIES // 2
    weights = ((downl_ref, down_ref), (upl_ref, up_ref))

    def shard_rows(d):
        return pl.ds(pl.multiple_of(d * shard, shard), shard)

    def across(w, k):
        local, full = weights[w]
        return pltpu.make_async_remote_copy(
            src_ref=local, dst_ref=full.at[shard_rows(dp_at)],
            send_sem=w_send.at[w, k], recv_sem=w_recv.at[w, k],
            device_id=(table_at, ((chip + k) % chips) * 2 + core), device_id_type=MESH,
        )

    def pass_on(w, k):
        local, full = weights[w]
        rows = shard_rows(((chip - k + chips) % chips) * 2 + core)
        return pltpu.make_async_remote_copy(
            src_ref=local if k == 0 else full.at[rows], dst_ref=full.at[rows],
            send_sem=c_send.at[w, k], recv_sem=c_recv.at[w, k],
            device_id=(table_at, chip * 2 + 1 - core), device_id_type=MESH,
        )

    own_weights = []
    for w in range(2):
        for k in (1, 3, 2):
            across(w, k).start()
        pass_on(w, 0).start()
        copy = pltpu.make_async_copy(
            weights[w][0], weights[w][1].at[shard_rows(dp_at)], l_sem.at[3 + w]
        )
        copy.start()
        own_weights.append(copy)

    confs = conf_ref.shape[0]
    versions = ver_ref[...]
    pair = jnp.concatenate(
        [(versions >> 7).astype(F32), (versions & 127).astype(F32)]
        + [jnp.zeros((6, versions.shape[1]), F32)], axis=0,
    ).astype(BF)
    local = loc_ref[...]
    line = lax.broadcasted_iota(jnp.int32, (LANES, confs), 0)

    def seen(k, carry):
        hit = jnp.where(line + k * LANES == local, 1.0, 0.0).astype(BF)
        hot2_ref[pl.ds(pl.multiple_of(k * LANES, LANES), LANES), 0:confs] = hit
        return carry

    lax.fori_loop(0, blocks, seen, 0)
    current = jnp.dot(pair, hot2_ref[:, 0:confs], preferred_element_type=F32)
    current = current[0:1, :] * 128.0 + current[1:2, :]
    newer = jnp.where(cver_ref[...].astype(F32) > current, 1.0, 0.0)
    conf = conf_ref[...]
    conf_high = conf.astype(BF)
    conf_low = (conf - conf_high.astype(F32)).astype(BF)
    fresh = jnp.concatenate([conf_high, conf_low, jnp.ones((confs, LANES), BF)], axis=1)

    def renew(k, carry):
        at = pl.ds(pl.multiple_of(k * LANES, LANES), LANES)
        mask = (hot2_ref[at, 0:confs].astype(F32) * newer).astype(BF)
        got = jnp.dot(mask, fresh, preferred_element_type=F32)
        now = table_ref[at, :]
        high = now.astype(BF).astype(F32)
        take = got[:, 2 * LANES : 3 * LANES] > 0.5
        tab_ref[at, 0:LANES] = jnp.where(take, got[:, 0:LANES], high).astype(BF)
        low = jnp.where(take, got[:, LANES : 2 * LANES], now - high)
        tab_ref[at, LANES : 2 * LANES] = low.astype(BF)
        return carry

    lax.fori_loop(0, blocks, renew, 0)

    own_request.wait()
    lane = lax.broadcasted_iota(jnp.int32, (SLOTS, LANES), 1)
    zero = jnp.zeros((SLOTS, LANES), BF)

    def chunk(ref, j):
        return ref.at[pl.ds(pl.multiple_of(j * SLOTS, SLOTS), SLOTS)]

    def answer_copy(j):
        return pltpu.make_async_remote_copy(
            src_ref=chunk(found_ref, j), dst_ref=chunk(ans_ref, j),
            send_sem=a_send.at[j], recv_sem=a_recv.at[j],
            device_id=(shifted(j, table_at, -1), dp_at), device_id_type=MESH,
        )

    own_answer = pltpu.make_async_copy(
        found_ref.at[0:SLOTS], ans_ref.at[0:SLOTS], l_sem.at[5]
    )

    def send_answers(g):
        for u in range(GROUP):
            j = g * GROUP + u
            if u == 0:

                @pl.when(j > 0)
                def _():
                    answer_copy(j).start()

            else:
                answer_copy(j).start()

    def answer_group(g, carry):
        lines = []
        for u in range(GROUP):
            j = g * GROUP + u
            if u == 0:

                @pl.when(j > 0)
                def _():
                    request_copy(j).wait_recv()

            else:
                request_copy(j).wait_recv()
            lines.append(asked_ref[j])
        columns = jnp.transpose(jnp.concatenate(lines, axis=0))
        for u in range(GROUP):
            low, high = [], []
            for q in range(2):
                at = 2 * u + q
                ids = jnp.broadcast_to(columns[0:SLOTS, at : at + 1], (SLOTS, LANES))
                low.append(jnp.where((ids & 127) == lane, 1.0, 0.0).astype(BF))
                high.append((ids >> 7).astype(F32).astype(BF))
            for k in range(blocks):
                k16 = BF(k)
                hot = jnp.where(high[0] == k16, low[0], zero) + jnp.where(
                    high[1] == k16, low[1], zero
                )
                hot_ref[u * SLOTS : (u + 1) * SLOTS, k * LANES : (k + 1) * LANES] = hot
        both = jnp.dot(hot_ref[...], tab_ref[...], preferred_element_type=F32)
        size = GROUP * SLOTS
        found_ref[pl.ds(pl.multiple_of(g * size, size), size), :] = (
            both[:, :LANES] + both[:, LANES:]
        ).astype(BF)

        @pl.when(g > 0)
        def _():
            send_answers(g - 1)

        return carry

    lax.fori_loop(0, PEERS // GROUP, answer_group, 0)
    own_answer.start()
    send_answers(PEERS // GROUP - 1)

    base_ref[:, :, 0:LANES] = dense_ref[...].astype(F32).reshape(samples // 8, 8, LANES)
    labels = jnp.broadcast_to(label_ref[...], (samples, samples)).astype(F32)
    labels = jnp.transpose(labels)[:, 0:1]
    for k in (1, 3, 2):
        for w in range(2):
            across(w, k).wait_recv()
            pass_on(w, k).start()
    own_answer.wait()
    rows_ref[0:SLOTS, :] = ans_ref[0:SLOTS, :].astype(F32)

    def take_answer(j, carry):
        answer_copy(j).wait_recv()
        at = pl.ds(pl.multiple_of(j * SLOTS, SLOTS), SLOTS)
        rows_ref[at, :] = ans_ref[at, :].astype(F32)
        return carry

    lax.fori_loop(1, PEERS, take_answer, 0)
    for copy in to_smem:
        copy.wait()

    def fetch(block, carry):
        b0 = block * 8
        for f in range(features):
            for u in range(8):
                row = rows_ref[pl.ds(pos_s[f, b0 + u], 1), :]
                base_ref[block, u : u + 1, (f + 1) * LANES : (f + 2) * LANES] = row
        return carry

    lax.fori_loop(0, samples // 8, fetch, 0)
    for w in range(2):
        own_weights[w].wait()
        for k in (0, 1, 3, 2):
            pass_on(w, k).wait_recv()
    inputs = base_ref[...].reshape(samples, width).astype(BF)
    crossed = lax.dot_general(inputs, down_ref[...], NT, preferred_element_type=F32).astype(BF)
    base = inputs.astype(F32)
    head = head_ref[...]
    factor = jnp.dot(crossed, up_ref[...], preferred_element_type=F32) + bias_ref[...]
    factor_ref[...] = factor
    logits = jnp.sum((base * factor + base) * head, axis=1, keepdims=True)
    logit_ref[...] = logits
    signal = loss_scale * (jax.nn.sigmoid(logits) - labels)
    state = signal * head
    lift = (state * base).astype(BF)
    cross = lax.dot_general(lift, up_ref[...], NT, preferred_element_type=F32).astype(BF)
    back = state + jnp.dot(cross, down_ref[...], preferred_element_type=F32) + state * factor_ref[...]
    for f in range(features):
        back_ref[f * samples : (f + 1) * samples, :] = back[:, (f + 1) * LANES : (f + 2) * LANES]

    def grad_copy(j):
        return pltpu.make_async_remote_copy(
            src_ref=gsend_ref.at[j], dst_ref=grecv_ref.at[j, pl.ds(0, SLOTS)],
            send_sem=g_send.at[j], recv_sem=g_recv.at[j],
            device_id=(shifted(j, table_at, 1), dp_at), device_id_type=MESH,
        )

    def place(i, carry):
        j = PEERS - 1 - i
        for r in range(SLOTS):
            stage_ref[r : r + 1, :] = back_ref[pl.ds(inv_s[j, r], 1), :]
        gsend_ref[j] = stage_ref[...].astype(BF)

        @pl.when(i > 0)
        def _():
            grad_copy(j + 1).start()

        return carry

    lax.fori_loop(0, PEERS, place, 0)
    own_grad = pltpu.make_async_copy(gsend_ref.at[0], grecv_ref.at[0, pl.ds(0, SLOTS)], l_sem.at[6])
    own_grad.start()

    spot = lax.broadcasted_iota(jnp.int32, (LANES, LANES), 0)
    nothing = jnp.zeros((LANES, LANES), BF)

    def hot_rows(j, u):
        both = asked_ref[j]
        low, high = [], []
        for q in range(2):
            ids = both[q : q + 1, :]
            low.append(jnp.where((ids & 127) == spot, 1.0, 0.0).astype(BF))
            wide = jnp.broadcast_to((ids >> 7).astype(F32), (LANES, LANES))
            high.append(wide.astype(BF))
        for k in range(blocks):
            k16 = BF(k)
            hot = jnp.where(high[0] == k16, low[0], nothing) + jnp.where(
                high[1] == k16, low[1], nothing
            )
            hot2_ref[k * LANES : (k + 1) * LANES, u * LANES : (u + 1) * LANES] = hot

    def take_group(i, carry):
        g = PEERS // GROUP - 1 - i
        for u in range(GROUP):
            hot_rows(g * GROUP + u, u)
        for u in range(GROUP - 1, -1, -1):
            j = g * GROUP + u
            if u == 0:

                @pl.when(j > 0)
                def _():
                    grad_copy(j).wait_recv()

            else:
                grad_copy(j).wait_recv()

        @pl.when(g == 0)
        def _():
            own_grad.wait()

        grads = grecv_ref[pl.ds(pl.multiple_of(g * GROUP, GROUP), GROUP)]
        grads = grads.reshape(GROUP * LANES, LANES)
        acc_ref[...] += jnp.dot(hot2_ref[...], grads, preferred_element_type=F32)
        return carry

    lax.fori_loop(0, PEERS // GROUP, take_group, 0)

    rsend_ref[...] = acc_ref[...].astype(BF)
    part_rows = out_ref.shape[0]

    def part_copy(k):
        target = (dp_at + k) % COPIES
        at = pl.ds(pl.multiple_of(target * part_rows, part_rows), part_rows)
        return pltpu.make_async_remote_copy(
            src_ref=rsend_ref.at[at], dst_ref=rrecv_ref.at[k],
            send_sem=r_send.at[k], recv_sem=r_recv.at[k],
            device_id=(table_at, target), device_id_type=MESH,
        )

    for k in (4, 3, 5, 2, 6, 1, 7):
        part_copy(k).start()
    result = acc_ref[pl.ds(pl.multiple_of(dp_at * part_rows, part_rows), part_rows), :]
    for k in (1, 7, 2, 6, 3, 5, 4):
        part_copy(k).wait_recv()
        result = result + rrecv_ref[k].astype(F32)
    out_ref[...] = result

    def drain(j, carry):
        request_copy(j).wait_send()
        answer_copy(j).wait_send()
        grad_copy(j).wait_send()
        return carry

    lax.fori_loop(1, PEERS, drain, 0)
    for w in range(2):
        for k in range(1, chips):
            across(w, k).wait_send()
        for k in range(chips):
            pass_on(w, k).wait_send()
    for k in range(1, COPIES):
        part_copy(k).wait_send()


def vspec():
    return pl.BlockSpec(memory_space=pltpu.VMEM)


def body(
    emb_table, versions, conf_local, conf_version, conf_values, owners, row_local, lengths,
    dense_out, labels, cross_down, cross_up, cross_bias, head_weight,
):
    rows_dev, emb_width = emb_table.shape
    samples, features, slot_count = row_local.shape
    width, shard = cross_down.shape[1:]
    rank = shard * COPIES
    bags = samples * features
    total = PEERS * SLOTS
    DMA = pltpu.SemaphoreType.DMA
    logits, emb_grad = pl.pallas_call(
        step_kernel,
        out_shape=(
            jax.ShapeDtypeStruct((samples, 1), F32),
            jax.ShapeDtypeStruct((rows_dev // COPIES, emb_width), F32),
        ),
        in_specs=[vspec()] * 14,
        out_specs=(vspec(), vspec()),
        scratch_shapes=[
            VM((features * PEERS, samples), BF),
            VM((features * PEERS, 2 * samples), F32),
            VM((PEERS, bags), BF),
            VM((PARTS * SLOTS, bags), BF),
            VM((PEERS, 2, LANES), jnp.int32),
            VM((PEERS, 2, LANES), jnp.int32),
            VM((features, samples), jnp.int32),
            VM((PEERS, LANES), jnp.int32),
            pltpu.SMEM((features, samples), jnp.int32),
            pltpu.SMEM((PEERS, LANES), jnp.int32),
            VM((rows_dev, 2 * LANES), BF),
            VM((GROUP * SLOTS, rows_dev), BF),
            VM((total, LANES), BF),
            VM((total, LANES), BF),
            VM((total, LANES), F32),
            VM((samples // 8, 8, width), F32),
            VM((samples, width), F32),
            VM((bags, LANES), F32),
            VM((rank, width), BF),
            VM((rank, width), BF),
            VM((SLOTS, LANES), F32),
            VM((PEERS, SLOTS, LANES), BF),
            VM((PEERS, LANES, LANES), BF),
            VM((rows_dev, GROUP * LANES), BF),
            VM((rows_dev, LANES), F32),
            VM((rows_dev, LANES), BF),
            VM((COPIES, rows_dev // COPIES, LANES), BF),
            DMA((PEERS,)), DMA((PEERS,)), DMA((PEERS,)), DMA((PEERS,)), DMA((PEERS,)), DMA((PEERS,)),
            DMA((2, 4)), DMA((2, 4)), DMA((2, 4)), DMA((2, 4)),
            DMA((COPIES,)), DMA((COPIES,)),
            DMA((7,)),
        ],
        compiler_params=pltpu.CompilerParams(
            collective_id=0, has_side_effects=True, vmem_limit_bytes=60 * 1024 * 1024
        ),
        name="step",
    )(
        owners.reshape(samples, features).T,
        jnp.transpose(row_local, (1, 2, 0)),
        lengths.T,
        versions.reshape(1, -1),
        conf_local.reshape(1, -1),
        conf_version.reshape(1, -1),
        emb_table,
        conf_values,
        dense_out,
        labels.reshape(1, -1),
        cross_down[0].T,
        cross_up[0],
        cross_bias,
        head_weight.reshape(1, -1),
    )
    return (logits.reshape(samples), emb_grad)


def solution(mesh):
    in_specs = (
        P("table", None),
        P("table"),
        P("table"),
        P("table"),
        P("table", None),
        P(("table", "dp"), None, None),
        P(("table", "dp"), None, None),
        P(("table", "dp"), None),
        P(("table", "dp"), None),
        P(("table", "dp")),
        P(None, None, "dp"),
        P(None, "dp", None),
        P(),
        P(),
    )
    out_specs = (P(("table", "dp")), P(("table", "dp"), None))
    return jax.shard_map(body, mesh=mesh, in_specs=in_specs, out_specs=out_specs, check_vma=False)
```

time: 678 us -> 174 us (0.26)
  waiting for transfers between devices: 392 us -> 0 us
  Pallas kernels: 0 us -> 168 us
  other arithmetic: 111 us -> 1.47 us
  local copies, waits for them, and re-layouts: 95.8 us -> 3.51 us
  starting transfers between devices: 51.7 us -> 0 us
  between operations: 14.2 us -> 0.65 us
  matrix products: 12.8 us -> 0 us
    all_to_all x4 -> x0, waiting for transfers between devices: 344 us -> none  [the longest x1 221 us: body(): lax.all_to_all(looked_up, 'table', split_axis=0, concat_axis=0, tiled=True)]
    pallas_call x0 -> x1, Pallas kernels: none -> 168 us  [body(): pl.pallas_call(step_kernel, out_shape=(jax.ShapeDtypeStruct((samples, 1),...]
    scatter-add x1 -> x0, other arithmetic: 63.2 us -> none  [body(): local_grad = jnp.zeros((rows_dev, emb_width), jnp.float32).at[got_rows.re...]
    all_to_all x4 -> x0, starting transfers between devices: 51.3 us -> none  [the longest x1 19.3 us: body(): lax.all_to_all(request_len, 'table', split_axis=0, concat_axis=0, tiled=T...]
    reduce_scatter x1 -> x0, waiting for transfers between devices: 46 us -> none  [body(): lax.psum_scatter(local_grad, 'dp', scatter_dimension=0, tiled=True)]
    scatter x4 -> x0, local copies, waits for them, and re-layouts: 44.3 us -> none  [the longest x2 17.5 us: body(): request_rows = jnp.zeros((peers * capacity, slot_count), jnp.int32).at[po...]
    gather x3 -> x0, local copies, waits for them, and re-layouts: 27.4 us -> none  [the longest x1 19.1 us: body(): looked_up = jnp.where(live_mask[..., None], updated[asked_rows], 0.0)]
    another operation x3 -> x0, other arithmetic: 19 us -> none
  transfers between devices with their start and end apart: 7 -> 0, of which waited for: 4 -> 0; matrix products, arithmetic and copies ran while one was open for 7% -> 0% of each run, Pallas kernels for 0% -> 0%
where the time goes in v2:
time: 174 us; the launch traced here: 173 us
  Pallas kernels  168 us (97%)
  local copies, waits for them, and re-layouts  3.51 us (2%)
    pallas_call x1, Pallas kernels, body(): pl.pallas_call(step_kernel, out_shape=(jax.ShapeDtypeStruct((samples, 1),...  168 us

profile of v2, /device:TPU:1, one launch (start us, length us, event | category | flops | bytes accessed | tf_op | source)
XLA Modules:
  0.0 173.4 jit_solution(9456919536723032992)
XLA Ops:
  0.6 0.0 copy-start
  0.6 1.3 reshape.30.head_ref
  2.0 0.0 copy-done
  2.0 0.6 copy.18
  2.6 167.8 %step.1 = (f32[128,1]{1,0:T(8,128)}, f32[256,128]{1,0:T(8,128)}) custom-call(s32[26,128]{1,0:T(8,128)} %bitcast.17, s32[26,2,128]{2,1,0:T(2,128)} %bitcast.18, s32[26,128]{1,0:T(8,128)} %bitcast.19, s32[1,2048]{1,0:T(1,128)} %bitcast.20, s32[1,256]{1,0:T(1,128)} %bitcast.21, s32[1,256]{1,0:T(1,128)} %bitcast.22, f32[2048,128]{1,0:T(8,128)} %table_ref.1, ...), custom_call_target="tpu_custom_call" | custom-call | tf_op jit(solution)/shard_map/step/pallas_call | solution.py:470
  170.4 1.5 reduce
  171.9 1.6 copy.20
Async XLA Ops:
  0.6 1.3 copy-start

commit v3 on v2

--- a/solution.py
+++ b/solution.py
@@ -11,6 +11,8 @@
 RING_Y = 4
 RING_Z = 16
 SLOTS = 80
+SENT = 78
+ASK = 4
 LANES = 128
 GROUP = 8
 DEAD = 2048
@@ -44,10 +46,10 @@
 
 
 def step_kernel(
-    own_ref, row_ref, len_ref, ver_ref, loc_ref, cver_ref, table_ref, conf_ref,
-    dense_ref, label_ref, downl_ref, upl_ref, bias_ref, head_ref,
+    own_ref, row_ref, len_ref, ver_ref, loc_ref, cver_ref, table_hbm, conf_hbm,
+    dense_ref, label_ref, downl_ref, upl_ref, bias_ref, heads_ref,
     logit_ref, out_ref,
-    hits_ref, prior_ref, wide_ref, placed_ref, req_ref, asked_ref, pos_v, inv_v, pos_s, inv_s,
+    own_s, head_ref, table_ref, conf_ref, hits_ref, prior_ref, wide_ref, placed_ref, req_ref, asked_ref, pos_v, inv_v, pos_s, inv_s,
     tab_ref, hot_ref, found_ref, ans_ref, rows_ref, base_ref, factor_ref, back_ref,
     down_ref, up_ref, stage_ref, gsend_ref, grecv_ref, hot2_ref, acc_ref, rsend_ref, rrecv_ref,
     q_send, q_recv, a_send, a_recv, g_send, g_recv, w_send, w_recv, c_send, c_recv, r_send, r_recv,
@@ -55,7 +57,7 @@
 ):
     table_at = lax.axis_index("table")
     dp_at = lax.axis_index("dp")
-    features, samples = own_ref.shape
+    features, samples = len_ref.shape
     total = PEERS * SLOTS
     width = bias_ref.shape[1]
     shard = downl_ref.shape[0]
@@ -70,24 +72,29 @@
         return carry
 
     lax.fori_loop(1, PEERS, greet, 0)
+    loads = [
+        pltpu.make_async_copy(table_hbm, table_ref, l_sem.at[7]),
+        pltpu.make_async_copy(conf_hbm, conf_ref, l_sem.at[8]),
+    ]
+    for load in loads:
+        load.start()
     for k in range(1, COPIES):
         pl.semaphore_signal(
             barrier, inc=1, device_id=(table_at, (dp_at + k) % COPIES), device_id_type=MESH
         )
 
-    grecv_ref[:, SLOTS:LANES, :] = jnp.zeros((PEERS, LANES - SLOTS, LANES), BF)
-    acc_ref[...] = jnp.zeros_like(acc_ref)
+    grecv_ref[:, SENT:LANES, :] = jnp.zeros((PEERS, LANES - SENT, LANES), BF)
+    own_s[...] = slot_of_owner(own_ref[:, 0, :], table_at)
 
     holder = lax.broadcasted_iota(jnp.int32, (PEERS, samples), 0)
 
     def mark_hits(f, carry):
-        hit = jnp.where(slot_of_owner(own_ref[pl.ds(f, 1), :], table_at) == holder, 1.0, 0.0)
-        hit = hit.astype(BF)
+        hit = jnp.where(own_s[pl.ds(f, 1), :] == holder, 1.0, 0.0).astype(BF)
         hits_ref[pl.ds(pl.multiple_of(f * PEERS, PEERS), PEERS), :] = hit
         wide_ref[:, pl.ds(pl.multiple_of(f * LANES, LANES), LANES)] = hit
         return carry
 
-    lax.fori_loop(0, features, mark_hits, 0)
+    lax.fori_loop(0, features, mark_hits, 0, unroll=13)
     row_at = lax.broadcasted_iota(jnp.int32, (samples, 2 * samples), 0)
     col_at = lax.broadcasted_iota(jnp.int32, (samples, 2 * samples), 1)
     before = jnp.where((row_at < col_at) | (col_at >= samples), 1.0, 0.0).astype(BF)
@@ -99,7 +106,7 @@
         at = pl.ds(pl.multiple_of(f * PEERS, PEERS), PEERS)
         onehot = hits_ref[at, :].astype(F32)
         rank = jnp.sum(onehot * (prior_ref[at, 0:samples] + carry), axis=0, keepdims=True)
-        owner = slot_of_owner(own_ref[pl.ds(f, 1), :], table_at)
+        owner = own_s[pl.ds(f, 1), :]
         pos_v[pl.ds(f, 1), :] = owner * SLOTS + jnp.clip(rank.astype(jnp.int32), 0, SLOTS - 1)
         both = row_ref[f]
         first = both[0:1, :]
@@ -110,7 +117,7 @@
         for value in (first, second):
             values.append((value >> 7).astype(F32))
             values.append((value & 127).astype(F32))
-        values.append(jnp.broadcast_to(f.astype(F32), (1, samples)))
+        values.append(jnp.full((1, samples), f, jnp.int32).astype(F32))
         values.append(sample)
         values.append(jnp.ones((1, samples), F32))
         for p, value in enumerate(values):
@@ -118,7 +125,7 @@
             placed_ref[p * SLOTS : (p + 1) * SLOTS, lanes] = placed
         return carry + prior_ref[at, samples : 2 * samples]
 
-    lax.fori_loop(0, features, rank_bags, jnp.zeros((PEERS, samples), F32))
+    lax.fori_loop(0, features, rank_bags, jnp.zeros((PEERS, samples), F32), unroll=13)
     packed = lax.dot_general(wide_ref[...], placed_ref[...], NT, preferred_element_type=F32)
     part = [packed[:, p * SLOTS : (p + 1) * SLOTS] for p in range(PARTS)]
     filled = part[6] > 0.5
@@ -205,6 +212,8 @@
         return carry
 
     lax.fori_loop(0, blocks, seen, 0)
+    for load in loads:
+        load.wait()
     current = jnp.dot(pair, hot2_ref[:, 0:confs], preferred_element_type=F32)
     current = current[0:1, :] * 128.0 + current[1:2, :]
     newer = jnp.where(cver_ref[...].astype(F32) > current, 1.0, 0.0)
@@ -232,7 +241,11 @@
     zero = jnp.zeros((SLOTS, LANES), BF)
 
     def chunk(ref, j):
-        return ref.at[pl.ds(pl.multiple_of(j * SLOTS, SLOTS), SLOTS)]
+        return ref.at[pl.ds(pl.multiple_of(j * SLOTS, SLOTS), SENT)]
+
+    def group_at(i):
+        late = (i + 3) // 8
+        return (1 - late) * (2 * i - 1) + late * (16 - 2 * i) + (8 - i) // 8
 
     def answer_copy(j):
         return pltpu.make_async_remote_copy(
@@ -242,36 +255,36 @@
         )
 
     own_answer = pltpu.make_async_copy(
-        found_ref.at[0:SLOTS], ans_ref.at[0:SLOTS], l_sem.at[5]
+        found_ref.at[0:SENT], ans_ref.at[0:SENT], l_sem.at[5]
     )
 
-    def send_answers(g):
-        for u in range(GROUP):
-            j = g * GROUP + u
-            if u == 0:
-
-                @pl.when(j > 0)
-                def _():
-                    answer_copy(j).start()
-
-            else:
-                answer_copy(j).start()
-
-    def answer_group(g, carry):
-        lines = []
-        for u in range(GROUP):
-            j = g * GROUP + u
-            if u == 0:
-
-                @pl.when(j > 0)
-                def _():
-                    request_copy(j).wait_recv()
-
-            else:
-                request_copy(j).wait_recv()
-            lines.append(asked_ref[j])
-        columns = jnp.transpose(jnp.concatenate(lines, axis=0))
-        for u in range(GROUP):
+    def first_slot(i):
+        per = GROUP // ASK
+        return group_at(i // per) * GROUP + (i % per) * ASK
+
+    def send_answers(i):
+        start = first_slot(i)
+
+        @pl.when(i > 0)
+        def _():
+            answer_copy(start).start()
+
+        for u in range(1, ASK):
+            answer_copy(start + u).start()
+
+    def answer_group(i, carry):
+        start = first_slot(i)
+
+        @pl.when(i > 0)
+        def _():
+            request_copy(start).wait_recv()
+
+        for u in range(1, ASK):
+            request_copy(start + u).wait_recv()
+        columns = jnp.transpose(
+            jnp.concatenate([asked_ref[start + u] for u in range(ASK)], axis=0)
+        )
+        for u in range(ASK):
             low, high = [], []
             for q in range(2):
                 at = 2 * u + q
@@ -285,21 +298,23 @@
                 )
                 hot_ref[u * SLOTS : (u + 1) * SLOTS, k * LANES : (k + 1) * LANES] = hot
         both = jnp.dot(hot_ref[...], tab_ref[...], preferred_element_type=F32)
-        size = GROUP * SLOTS
-        found_ref[pl.ds(pl.multiple_of(g * size, size), size), :] = (
+        found_ref[pl.ds(pl.multiple_of(start * SLOTS, SLOTS), ASK * SLOTS), :] = (
             both[:, :LANES] + both[:, LANES:]
         ).astype(BF)
 
-        @pl.when(g > 0)
+        @pl.when(i > 0)
         def _():
-            send_answers(g - 1)
-
-        return carry
-
-    lax.fori_loop(0, PEERS // GROUP, answer_group, 0)
+            send_answers(i - 1)
+
+        return carry
+
+    lax.fori_loop(0, PEERS // ASK, answer_group, 0)
     own_answer.start()
-    send_answers(PEERS // GROUP - 1)
-
+    send_answers(jnp.int32(PEERS // ASK - 1))
+
+    acc_ref[...] = jnp.zeros_like(acc_ref)
+    for f in range(features + 1):
+        head_ref[:, f * LANES : (f + 1) * LANES] = heads_ref[f : f + 1, :]
     base_ref[:, :, 0:LANES] = dense_ref[...].astype(F32).reshape(samples // 8, 8, LANES)
     labels = jnp.broadcast_to(label_ref[...], (samples, samples)).astype(F32)
     labels = jnp.transpose(labels)[:, 0:1]
@@ -340,7 +355,7 @@
     factor = jnp.dot(crossed, up_ref[...], preferred_element_type=F32) + bias_ref[...]
     factor_ref[...] = factor
     logits = jnp.sum((base * factor + base) * head, axis=1, keepdims=True)
-    logit_ref[...] = logits
+    logit_ref[...] = jnp.transpose(jnp.broadcast_to(logits, (samples, samples)))[0:1, :]
     signal = loss_scale * (jax.nn.sigmoid(logits) - labels)
     state = signal * head
     lift = (state * base).astype(BF)
@@ -351,7 +366,7 @@
 
     def grad_copy(j):
         return pltpu.make_async_remote_copy(
-            src_ref=gsend_ref.at[j], dst_ref=grecv_ref.at[j, pl.ds(0, SLOTS)],
+            src_ref=gsend_ref.at[j, pl.ds(0, SENT)], dst_ref=grecv_ref.at[j, pl.ds(0, SENT)],
             send_sem=g_send.at[j], recv_sem=g_recv.at[j],
             device_id=(shifted(j, table_at, 1), dp_at), device_id_type=MESH,
         )
@@ -369,7 +384,9 @@
         return carry
 
     lax.fori_loop(0, PEERS, place, 0)
-    own_grad = pltpu.make_async_copy(gsend_ref.at[0], grecv_ref.at[0, pl.ds(0, SLOTS)], l_sem.at[6])
+    own_grad = pltpu.make_async_copy(
+        gsend_ref.at[0, pl.ds(0, SENT)], grecv_ref.at[0, pl.ds(0, SENT)], l_sem.at[6]
+    )
     own_grad.start()
 
     spot = lax.broadcasted_iota(jnp.int32, (LANES, LANES), 0)
@@ -390,47 +407,52 @@
             )
             hot2_ref[k * LANES : (k + 1) * LANES, u * LANES : (u + 1) * LANES] = hot
 
+    def grads_of(g):
+        for u in range(GROUP):
+            hot_rows(g * GROUP + u, u)
+        for u in range(GROUP - 1, 0, -1):
+            grad_copy(g * GROUP + u).wait_recv()
+
+    def group_rows(g):
+        grads = grecv_ref[pl.ds(pl.multiple_of(g * GROUP, GROUP), GROUP)]
+        return grads.reshape(GROUP * LANES, LANES)
+
     def take_group(i, carry):
         g = PEERS // GROUP - 1 - i
-        for u in range(GROUP):
-            hot_rows(g * GROUP + u, u)
-        for u in range(GROUP - 1, -1, -1):
-            j = g * GROUP + u
-            if u == 0:
-
-                @pl.when(j > 0)
-                def _():
-                    grad_copy(j).wait_recv()
-
-            else:
-                grad_copy(j).wait_recv()
-
-        @pl.when(g == 0)
-        def _():
-            own_grad.wait()
-
-        grads = grecv_ref[pl.ds(pl.multiple_of(g * GROUP, GROUP), GROUP)]
-        grads = grads.reshape(GROUP * LANES, LANES)
-        acc_ref[...] += jnp.dot(hot2_ref[...], grads, preferred_element_type=F32)
-        return carry
-
-    lax.fori_loop(0, PEERS // GROUP, take_group, 0)
-
-    rsend_ref[...] = acc_ref[...].astype(BF)
+        grads_of(g)
+        grad_copy(g * GROUP).wait_recv()
+        acc_ref[...] += jnp.dot(hot2_ref[...], group_rows(g), preferred_element_type=F32)
+        return carry
+
+    lax.fori_loop(0, PEERS // GROUP - 1, take_group, 0)
+    grads_of(0)
+    own_grad.wait()
+
     part_rows = out_ref.shape[0]
+    last = grecv_ref[0:GROUP].reshape(GROUP * LANES, LANES)
+
+    def part_at(k):
+        target = (dp_at + k) % COPIES
+        return pl.ds(pl.multiple_of(target * part_rows, part_rows), part_rows)
 
     def part_copy(k):
-        target = (dp_at + k) % COPIES
-        at = pl.ds(pl.multiple_of(target * part_rows, part_rows), part_rows)
         return pltpu.make_async_remote_copy(
-            src_ref=rsend_ref.at[at], dst_ref=rrecv_ref.at[k],
+            src_ref=rsend_ref.at[part_at(k)], dst_ref=rrecv_ref.at[k],
             send_sem=r_send.at[k], recv_sem=r_recv.at[k],
-            device_id=(table_at, target), device_id_type=MESH,
-        )
-
-    for k in (4, 3, 5, 2, 6, 1, 7):
-        part_copy(k).start()
-    result = acc_ref[pl.ds(pl.multiple_of(dp_at * part_rows, part_rows), part_rows), :]
+            device_id=(table_at, (dp_at + k) % COPIES), device_id_type=MESH,
+        )
+
+    def part_sum(k):
+        at = part_at(k)
+        return acc_ref[at, :] + jnp.dot(hot2_ref[at, :], last, preferred_element_type=F32)
+
+    order = (4, 3, 5, 2, 6, 1, 7)
+    for n, k in enumerate(order):
+        rsend_ref[part_at(k), :] = part_sum(k).astype(BF)
+        if n > 0:
+            part_copy(order[n - 1]).start()
+    result = part_sum(0)
+    part_copy(order[-1]).start()
     for k in (1, 7, 2, 6, 3, 5, 4):
         part_copy(k).wait_recv()
         result = result + rrecv_ref[k].astype(F32)
@@ -467,15 +489,20 @@
     bags = samples * features
     total = PEERS * SLOTS
     DMA = pltpu.SemaphoreType.DMA
+    hbm = pl.BlockSpec(memory_space=pl.ANY)
     logits, emb_grad = pl.pallas_call(
         step_kernel,
         out_shape=(
-            jax.ShapeDtypeStruct((samples, 1), F32),
+            jax.ShapeDtypeStruct((1, samples), F32),
             jax.ShapeDtypeStruct((rows_dev // COPIES, emb_width), F32),
         ),
-        in_specs=[vspec()] * 14,
+        in_specs=[vspec()] * 6 + [hbm, hbm] + [vspec()] * 2 + [hbm, hbm] + [vspec()] * 2,
         out_specs=(vspec(), vspec()),
         scratch_shapes=[
+            VM((features, samples), jnp.int32),
+            VM((1, width), F32),
+            VM((rows_dev, LANES), F32),
+            VM((conf_local.shape[0], LANES), F32),
             VM((features * PEERS, samples), BF),
             VM((features * PEERS, 2 * samples), F32),
             VM((PEERS, bags), BF),
@@ -487,7 +514,7 @@
             pltpu.SMEM((features, samples), jnp.int32),
             pltpu.SMEM((PEERS, LANES), jnp.int32),
             VM((rows_dev, 2 * LANES), BF),
-            VM((GROUP * SLOTS, rows_dev), BF),
+            VM((ASK * SLOTS, rows_dev), BF),
             VM((total, LANES), BF),
             VM((total, LANES), BF),
             VM((total, LANES), F32),
@@ -506,14 +533,14 @@
             DMA((PEERS,)), DMA((PEERS,)), DMA((PEERS,)), DMA((PEERS,)), DMA((PEERS,)), DMA((PEERS,)),
             DMA((2, 4)), DMA((2, 4)), DMA((2, 4)), DMA((2, 4)),
             DMA((COPIES,)), DMA((COPIES,)),
-            DMA((7,)),
+            DMA((9,)),
         ],
         compiler_params=pltpu.CompilerParams(
             collective_id=0, has_side_effects=True, vmem_limit_bytes=60 * 1024 * 1024
         ),
         name="step",
     )(
-        owners.reshape(samples, features).T,
+        jnp.transpose(owners, (1, 2, 0)),
         jnp.transpose(row_local, (1, 2, 0)),
         lengths.T,
         versions.reshape(1, -1),
@@ -526,7 +553,7 @@
         cross_down[0].T,
         cross_up[0],
         cross_bias,
-        head_weight.reshape(1, -1),
+        head_weight.reshape(-1, LANES),
     )
     return (logits.reshape(samples), emb_grad)
 

time: 174 us -> 168 us (0.966)
  Pallas kernels: 168 us -> 164 us
    pallas_call x1, Pallas kernels: 168 us -> 164 us  [body(): pl.pallas_call(step_kernel, out_shape=(jax.ShapeDtypeStruct((1, samples),...]
where the time goes in v3:
time: 168 us; the launch traced here: 167 us
  Pallas kernels  164 us (98%)
  local copies, waits for them, and re-layouts  2.72 us (2%)
    pallas_call x1, Pallas kernels, body(): pl.pallas_call(step_kernel, out_shape=(jax.ShapeDtypeStruct((1, samples),...  164 us

profile of v3, /device:TPU:1, one launch (start us, length us, event | category | flops | bytes accessed | tf_op | source)
XLA Modules:
  0.0 167.5 jit_solution(11591113944109937780)
XLA Ops:
  0.6 164.1 %step.1 = (f32[1,128]{1,0:T(1,128)}, f32[256,128]{1,0:T(8,128)}) custom-call(s32[26,1,128]{2,1,0:T(1,128)} %bitcast.18, s32[26,2,128]{2,1,0:T(2,128)} %bitcast.15, s32[26,128]{1,0:T(8,128)} %bitcast.16, s32[1,2048]{1,0:T(1,128)} %bitcast.19, s32[1,256]{1,0:T(1,128)} %bitcast.20, s32[1,256]{1,0:T(1,128)} %bitcast.21, f32[2048,128]{1,0:T(8,128)} %table_hbm.1, ...), custom_call_target="tpu_custom_call" | custom-call | tf_op jit(solution)/shard_map/step/pallas_call | solution.py:493
  164.7 0.0 copy-start
  164.7 0.6 copy-done
  165.4 0.5 copy.18
  165.9 1.6 copy.19
Async XLA Ops:
  164.7 0.7 copy-start

commit v4 on v3

--- a/solution.py
+++ b/solution.py
@@ -12,7 +12,7 @@
 RING_Z = 16
 SLOTS = 80
 SENT = 78
-ASK = 4
+ASK = 2
 LANES = 128
 GROUP = 8
 DEAD = 2048
@@ -46,18 +46,19 @@
 
 
 def step_kernel(
-    own_ref, row_ref, len_ref, ver_ref, loc_ref, cver_ref, table_hbm, conf_hbm,
-    dense_ref, label_ref, downl_ref, upl_ref, bias_ref, heads_ref,
+    own_hbm, row_hbm, len_hbm, ver_hbm, loc_hbm, cver_hbm, table_hbm, conf_hbm,
+    dense_hbm, label_hbm, downl_ref, upl_ref, bias_hbm, heads_hbm,
     logit_ref, out_ref,
+    own_ref, row_ref, len_ref, ver_ref, loc_ref, cver_ref, dense_ref, label_ref, bias_ref, heads_ref,
     own_s, head_ref, table_ref, conf_ref, hits_ref, prior_ref, wide_ref, placed_ref, req_ref, asked_ref, pos_v, inv_v, pos_s, inv_s,
     tab_ref, hot_ref, found_ref, ans_ref, rows_ref, base_ref, factor_ref, back_ref,
-    down_ref, up_ref, stage_ref, gsend_ref, grecv_ref, hot2_ref, acc_ref, rsend_ref, rrecv_ref,
+    down_ref, up_ref, stage_ref, gsend_ref, grecv_ref, hot2_ref, acc_ref, rown_ref, rsend_ref, rrecv_ref,
     q_send, q_recv, a_send, a_recv, g_send, g_recv, w_send, w_recv, c_send, c_recv, r_send, r_recv,
     l_sem,
 ):
     table_at = lax.axis_index("table")
     dp_at = lax.axis_index("dp")
-    features, samples = len_ref.shape
+    features, samples = len_hbm.shape
     total = PEERS * SLOTS
     width = bias_ref.shape[1]
     shard = downl_ref.shape[0]
@@ -65,25 +66,36 @@
 
     barrier = pltpu.get_barrier_semaphore()
 
-    def greet(j, carry):
+    def greet(i, carry):
         pl.semaphore_signal(
-            barrier, inc=1, device_id=(shifted(j, table_at, 1), dp_at), device_id_type=MESH
+            barrier, inc=1, device_id=(shifted(PEERS - i, table_at, 1), dp_at), device_id_type=MESH
         )
         return carry
 
     lax.fori_loop(1, PEERS, greet, 0)
+    core, chip = dp_at % 2, dp_at // 2
+    chips = COPIES // 2
+    for k in range(1, chips):
+        pl.semaphore_signal(
+            barrier, inc=1, device_id=(table_at, ((chip + k) % chips) * 2 + core),
+            device_id_type=MESH,
+        )
+    pl.semaphore_signal(
+        barrier, inc=1, device_id=(table_at, chip * 2 + 1 - core), device_id_type=MESH
+    )
+    sources = (
+        (own_hbm, own_ref), (row_hbm, row_ref), (len_hbm, len_ref), (ver_hbm, ver_ref),
+        (loc_hbm, loc_ref), (cver_hbm, cver_ref), (dense_hbm, dense_ref), (label_hbm, label_ref),
+        (bias_hbm, bias_ref), (heads_hbm, heads_ref), (table_hbm, table_ref), (conf_hbm, conf_ref),
+    )
     loads = [
-        pltpu.make_async_copy(table_hbm, table_ref, l_sem.at[7]),
-        pltpu.make_async_copy(conf_hbm, conf_ref, l_sem.at[8]),
+        pltpu.make_async_copy(src, dst, l_sem.at[7 + n]) for n, (src, dst) in enumerate(sources)
     ]
     for load in loads:
         load.start()
-    for k in range(1, COPIES):
-        pl.semaphore_signal(
-            barrier, inc=1, device_id=(table_at, (dp_at + k) % COPIES), device_id_type=MESH
-        )
-
     grecv_ref[:, SENT:LANES, :] = jnp.zeros((PEERS, LANES - SENT, LANES), BF)
+    for load in loads[:3]:
+        load.wait()
     own_s[...] = slot_of_owner(own_ref[:, 0, :], table_at)
 
     holder = lax.broadcasted_iota(jnp.int32, (PEERS, samples), 0)
@@ -147,7 +159,7 @@
     own_request = pltpu.make_async_copy(req_ref.at[0], asked_ref.at[0], l_sem.at[2])
     own_request.start()
 
-    pl.semaphore_wait(barrier, PEERS - 1 + COPIES - 1)
+    pl.semaphore_wait(barrier, PEERS - 1 + chips)
 
     def request_copy(j):
         return pltpu.make_async_remote_copy(
@@ -156,14 +168,12 @@
             device_id=(shifted(j, table_at, 1), dp_at), device_id_type=MESH,
         )
 
-    def send_request(j, carry):
-        request_copy(j).start()
+    def send_request(i, carry):
+        request_copy(PEERS - i).start()
         return carry
 
     lax.fori_loop(1, PEERS, send_request, 0)
 
-    core, chip = dp_at % 2, dp_at // 2
-    chips = COPIES // 2
     weights = ((downl_ref, down_ref), (upl_ref, up_ref))
 
     def shard_rows(d):
@@ -197,6 +207,8 @@
         copy.start()
         own_weights.append(copy)
 
+    for load in loads[3:]:
+        load.wait()
     confs = conf_ref.shape[0]
     versions = ver_ref[...]
     pair = jnp.concatenate(
@@ -212,8 +224,6 @@
         return carry
 
     lax.fori_loop(0, blocks, seen, 0)
-    for load in loads:
-        load.wait()
     current = jnp.dot(pair, hot2_ref[:, 0:confs], preferred_element_type=F32)
     current = current[0:1, :] * 128.0 + current[1:2, :]
     newer = jnp.where(cver_ref[...].astype(F32) > current, 1.0, 0.0)
@@ -355,7 +365,7 @@
     factor = jnp.dot(crossed, up_ref[...], preferred_element_type=F32) + bias_ref[...]
     factor_ref[...] = factor
     logits = jnp.sum((base * factor + base) * head, axis=1, keepdims=True)
-    logit_ref[...] = jnp.transpose(jnp.broadcast_to(logits, (samples, samples)))[0:1, :]
+    logit_ref[...] = jnp.transpose(jnp.broadcast_to(logits, (samples, samples)))[0, :]
     signal = loss_scale * (jax.nn.sigmoid(logits) - labels)
     state = signal * head
     lift = (state * base).astype(BF)
@@ -388,6 +398,18 @@
         gsend_ref.at[0, pl.ds(0, SENT)], grecv_ref.at[0, pl.ds(0, SENT)], l_sem.at[6]
     )
     own_grad.start()
+
+    def drain(j, carry):
+        request_copy(j).wait_send()
+        answer_copy(j).wait_send()
+        return carry
+
+    lax.fori_loop(1, PEERS, drain, 0)
+    for w in range(2):
+        for k in range(1, chips):
+            across(w, k).wait_send()
+        for k in range(chips):
+            pass_on(w, k).wait_send()
 
     spot = lax.broadcasted_iota(jnp.int32, (LANES, LANES), 0)
     nothing = jnp.zeros((LANES, LANES), BF)
@@ -422,6 +444,8 @@
         grads_of(g)
         grad_copy(g * GROUP).wait_recv()
         acc_ref[...] += jnp.dot(hot2_ref[...], group_rows(g), preferred_element_type=F32)
+        for u in range(GROUP):
+            grad_copy(g * GROUP + u).wait_send()
         return carry
 
     lax.fori_loop(0, PEERS // GROUP - 1, take_group, 0)
@@ -431,47 +455,55 @@
     part_rows = out_ref.shape[0]
     last = grecv_ref[0:GROUP].reshape(GROUP * LANES, LANES)
 
-    def part_at(k):
-        target = (dp_at + k) % COPIES
+    def part_at(k, side):
+        target = ((chip + k) % chips) * 2 + side
         return pl.ds(pl.multiple_of(target * part_rows, part_rows), part_rows)
 
-    def part_copy(k):
+    def part_sum(k, side):
+        at = part_at(k, side)
+        return acc_ref[at, :] + jnp.dot(hot2_ref[at, :], last, preferred_element_type=F32)
+
+    def beside(k):
         return pltpu.make_async_remote_copy(
-            src_ref=rsend_ref.at[part_at(k)], dst_ref=rrecv_ref.at[k],
+            src_ref=rsend_ref.at[k], dst_ref=rrecv_ref.at[k],
             send_sem=r_send.at[k], recv_sem=r_recv.at[k],
-            device_id=(table_at, (dp_at + k) % COPIES), device_id_type=MESH,
-        )
-
-    def part_sum(k):
-        at = part_at(k)
-        return acc_ref[at, :] + jnp.dot(hot2_ref[at, :], last, preferred_element_type=F32)
-
-    order = (4, 3, 5, 2, 6, 1, 7)
+            device_id=(table_at, chip * 2 + 1 - core), device_id_type=MESH,
+        )
+
+    def along(k):
+        return pltpu.make_async_remote_copy(
+            src_ref=rsend_ref.at[chips + k], dst_ref=rrecv_ref.at[chips + k],
+            send_sem=r_send.at[chips + k], recv_sem=r_recv.at[chips + k],
+            device_id=(table_at, ((chip + k) % chips) * 2 + core), device_id_type=MESH,
+        )
+
+    order = (2, 3, 1, 0)
     for n, k in enumerate(order):
-        rsend_ref[part_at(k), :] = part_sum(k).astype(BF)
+        rsend_ref[k] = part_sum(k, 1 - core).astype(BF)
         if n > 0:
-            part_copy(order[n - 1]).start()
-    result = part_sum(0)
-    part_copy(order[-1]).start()
-    for k in (1, 7, 2, 6, 3, 5, 4):
-        part_copy(k).wait_recv()
-        result = result + rrecv_ref[k].astype(F32)
+            beside(order[n - 1]).start()
+    for n, k in enumerate(order):
+        rown_ref[k] = part_sum(k, core)
+        if n == 0:
+            beside(order[-1]).start()
+    for n, k in enumerate(order):
+        beside(k).wait_recv()
+        both = rown_ref[k] + rrecv_ref[k].astype(F32)
+        if n > 0:
+            along(order[n - 1]).start()
+        if k > 0:
+            rsend_ref[chips + k] = both.astype(BF)
+    result = both
+    for u in range(1, GROUP):
+        grad_copy(u).wait_send()
+    for k in range(chips):
+        beside(k).wait_send()
+    for k in (1, 3, 2):
+        along(k).wait_recv()
+        result = result + rrecv_ref[chips + k].astype(F32)
     out_ref[...] = result
-
-    def drain(j, carry):
-        request_copy(j).wait_send()
-        answer_copy(j).wait_send()
-        grad_copy(j).wait_send()
-        return carry
-
-    lax.fori_loop(1, PEERS, drain, 0)
-    for w in range(2):
-        for k in range(1, chips):
-            across(w, k).wait_send()
-        for k in range(chips):
-            pass_on(w, k).wait_send()
-    for k in range(1, COPIES):
-        part_copy(k).wait_send()
+    for k in range(1, chips):
+        along(k).wait_send()
 
 
 def vspec():
@@ -493,12 +525,22 @@
     logits, emb_grad = pl.pallas_call(
         step_kernel,
         out_shape=(
-            jax.ShapeDtypeStruct((1, samples), F32),
+            jax.ShapeDtypeStruct((samples,), F32),
             jax.ShapeDtypeStruct((rows_dev // COPIES, emb_width), F32),
         ),
-        in_specs=[vspec()] * 6 + [hbm, hbm] + [vspec()] * 2 + [hbm, hbm] + [vspec()] * 2,
+        in_specs=[hbm] * 14,
         out_specs=(vspec(), vspec()),
         scratch_shapes=[
+            VM((features, 1, samples), jnp.int32),
+            VM((features, slot_count, samples), jnp.int32),
+            VM((features, samples), jnp.int32),
+            VM((1, rows_dev), jnp.int32),
+            VM((1, conf_local.shape[0]), jnp.int32),
+            VM((1, conf_local.shape[0]), jnp.int32),
+            VM(dense_out.shape, BF),
+            VM((1, samples), jnp.int32),
+            VM((1, width), F32),
+            VM((width // LANES, LANES), F32),
             VM((features, samples), jnp.int32),
             VM((1, width), F32),
             VM((rows_dev, LANES), F32),
@@ -528,12 +570,13 @@
             VM((PEERS, LANES, LANES), BF),
             VM((rows_dev, GROUP * LANES), BF),
             VM((rows_dev, LANES), F32),
-            VM((rows_dev, LANES), BF),
+            VM((COPIES // 2, rows_dev // COPIES, LANES), F32),
+            VM((COPIES, rows_dev // COPIES, LANES), BF),
             VM((COPIES, rows_dev // COPIES, LANES), BF),
             DMA((PEERS,)), DMA((PEERS,)), DMA((PEERS,)), DMA((PEERS,)), DMA((PEERS,)), DMA((PEERS,)),
             DMA((2, 4)), DMA((2, 4)), DMA((2, 4)), DMA((2, 4)),
             DMA((COPIES,)), DMA((COPIES,)),
-            DMA((9,)),
+            DMA((19,)),
         ],
         compiler_params=pltpu.CompilerParams(
             collective_id=0, has_side_effects=True, vmem_limit_bytes=60 * 1024 * 1024
@@ -555,7 +598,7 @@
         cross_bias,
         head_weight.reshape(-1, LANES),
     )
-    return (logits.reshape(samples), emb_grad)
+    return (logits, emb_grad)
 
 
 def solution(mesh):

time: 168 us -> 167 us (level)
  no operation moved by 1% of the time
where the time goes in v4:
time: 167 us
  Pallas kernels  164 us (98%)
  local copies, waits for them, and re-layouts  2.72 us (2%)
    pallas_call x1, Pallas kernels, body(): pl.pallas_call(step_kernel, out_shape=(jax.ShapeDtypeStruct((samples,), F...  164 us

profile of v4, /device:TPU:1, one launch (start us, length us, event | category | flops | bytes accessed | tf_op | source)
XLA Modules:
  0.0 167.1 jit_solution(7363175931619042158)
XLA Ops:
  0.6 163.7 %step.1 = (f32[128]{0:T(128)}, f32[256,128]{1,0:T(8,128)}) custom-call(s32[26,1,128]{2,1,0:T(1,128)} %bitcast.17, s32[26,2,128]{2,1,0:T(2,128)} %bitcast.14, s32[26,128]{1,0:T(8,128)} %bitcast.15, s32[1,2048]{1,0:T(1,128)} %bitcast.18, s32[1,256]{1,0:T(1,128)} %bitcast.19, s32[1,256]{1,0:T(1,128)} %bitcast.20, f32[2048,128]{1,0:T(8,128)} %table_hbm.1, ...), custom_call_target="tpu_custom_call" | custom-call | tf_op jit(solution)/shard_map/step/pallas_call | solution.py:525
  164.3 0.0 copy-start
  164.3 0.6 copy-done
  165.0 0.5 copy.18
  165.5 1.6 copy.19
Async XLA Ops:
  164.3 0.7 copy-start

commit v5 on v4

--- a/solution.py
+++ b/solution.py
@@ -579,7 +579,7 @@
             DMA((19,)),
         ],
         compiler_params=pltpu.CompilerParams(
-            collective_id=0, has_side_effects=True, vmem_limit_bytes=60 * 1024 * 1024
+            collective_id=0, has_side_effects=True, vmem_limit_bytes=50 << 20
         ),
         name="step",
     )(

time: 167 us -> 175 us (1.048)
  local copies, waits for them, and re-layouts: 2.72 us -> 10.3 us
    unnamed x4 -> x30, local copies, waits for them, and re-layouts: 2.72 us -> 10.3 us
where the time goes in v5:
time: 175 us
  Pallas kernels  164 us (94%)
  local copies, waits for them, and re-layouts  10.3 us (6%)
    pallas_call x1, Pallas kernels, body(): pl.pallas_call(step_kernel, out_shape=(jax.ShapeDtypeStruct((samples,), F...  164 us
    unnamed x30, local copies, waits for them, and re-layouts  10.3 us

profile of v5, /device:TPU:1, one launch (start us, length us, event | category | flops | bytes accessed | tf_op | source)
XLA Modules:
  0.0 174.7 jit_solution(6960838962552921017)
XLA Ops:
  0.6 0.0 copy-start.6
  0.6 0.0 copy-start.12
  0.7 0.0 copy-start.11
  0.7 0.0 copy-start.13
  0.7 0.7 copy-done.6
  1.4 0.0 copy-done.12
  1.4 0.0 copy-done.11
  1.4 0.0 copy-done.13
  1.4 0.0 copy-start
  1.4 1.2 copy-done
  2.6 0.0 copy-start.1
  2.6 1.0 copy-done.1
  3.6 0.0 copy-start.2
  3.6 1.0 copy-done.2
  4.6 0.0 copy-start.3
  4.6 0.9 copy-done.3
  5.5 0.0 copy-start.4
  5.5 0.8 copy-done.4
  6.3 0.0 copy-start.5
  6.3 0.7 copy-done.5
  7.0 0.0 copy-start.7
  7.0 0.7 copy-done.7
  7.7 0.0 copy-start.8
  7.7 0.7 copy-done.8
  8.5 0.0 copy-start.9
  8.5 0.7 copy-done.9
  9.2 0.0 copy-start.10
  9.2 0.7 copy-done.10
  9.9 163.7 %step.1 = (f32[128]{0:T(128)S(1)}, f32[256,128]{1,0:T(8,128)S(1)}) custom-call(s32[26,1,128]{2,1,0:T(1,128)S(1)} %bitcast.17, s32[26,2,128]{2,1,0:T(2,128)S(1)} %bitcast.14, s32[26,128]{1,0:T(8,128)S(1)} %bitcast.15, s32[1,2048]{1,0:T(1,128)S(1)} %bitcast.18, s32[1,256]{1,0:T(1,128)S(1)} %bitcast.19, s32[1,256]{1,0:T(1,128)S(1)} %bitcast.20, ...), custom_call_target="tpu_custom_call" | custom-call | tf_op jit(solution)/shard_map/step/pallas_call | solution.py:525
  173.6 0.5 copy.18
  174.1 0.7 copy.19
Async XLA Ops:
  0.6 0.7 copy-start.6
  0.6 0.7 copy-start.12
  0.7 0.7 copy-start.11
  0.7 0.7 copy-start.13
  1.4 1.2 copy-start
  2.6 1.0 copy-start.1
  3.6 1.0 copy-start.2
  4.6 0.9 copy-start.3
  5.5 0.8 copy-start.4
  6.3 0.7 copy-start.5
  7.0 0.7 copy-start.7
  7.7 0.7 copy-start.8
  8.5 0.7 copy-start.9
  9.2 0.7 copy-start.10
